TPU v7x, 256 devices: a whole 4x4x8 slice. The times are simulated.
256 devices in a mesh: dp: 32 (over z, y), fsdp: 8 (over x, core).
Axes of the slice: x: 4, y: 4, z: 8, core: 2. Of those that a mesh axis runs over, the one named last changes fastest.
Arguments:
- waveform: bfloat16 [8, 960, 1280], P('fsdp', 'dp'), may hold values from -6 to 6
- clip_lengths: int32 [8, 32, 1], replicated, may hold values from 320 to 38400, as said below
- conv_first: bfloat16 [10, 512], replicated, may hold values from -2 to 2
- conv_mid: bfloat16 [4, 3, 512, 512], replicated, may hold values from -0.15625 to 0.15625
- conv_last: bfloat16 [2, 2, 512, 512], replicated, may hold values from -0.1875 to 0.1875
- conv_gain: float32 [7, 512], replicated, may hold values from 0.1 to 1.9
- conv_shift: float32 [7, 512], replicated, may hold values from -1.5 to 1.5
- proj_gain: float32 [512], replicated, may hold values from 0.1 to 1.9
- proj_shift: float32 [512], replicated, may hold values from -1.5 to 1.5
- proj_weight: bfloat16 [512, 1280], replicated, may hold values from -0.25 to 0.25
- proj_bias: float32 [1280], replicated, may hold values from -1.5 to 1.5
- pos_weight: bfloat16 [16, 128, 80, 80], P('fsdp'), may hold values from -0.0625 to 0.0625
- pos_bias: float32 [1280], replicated, may hold values from -1.5 to 1.5
Outputs:
- features: bfloat16 [8, 2048, 1280], P('fsdp', 'dp')
Inputs may be any that keep to these rules, and one draw needn't show every extreme that they name: `clip_lengths`: every length is a positive multiple of 320. The lengths of one source sum to 1280 times a whole number of blocks, at most 30; the block counts of one clip batch total 32 * 16, and in every clip batch some source holds exactly 30 blocks.
All inputs are finite; a program needn't handle non-finite values.
Results may differ from a plain program's by a relative error of at most 0.015.
Values may be sent and summed in bfloat16 or wider, within the bound.
A program may use at most 192 MiB of HBM per device.

v0:
```python
import jax
import jax.numpy as jnp
from jax import lax
from jax.sharding import PartitionSpec as P
from jax.experimental import pallas as pl
from jax.experimental.pallas import tpu as pltpu

NORM_EPS = 1e-5
R2 = 0.7071067811865476

TAPS = 128
FPB = 4
NB = 16


def padded_2(value, sides, width):
    for axis, dim in sides:
        size, length = (lax.axis_size(axis), value.shape[dim])
        up = [(i, (i + 1) % size) for i in range(size - 1)]
        down = [(j, i) for i, j in up]
        last = lax.slice_in_dim(value, length - width, length, axis=dim)
        leading = lax.slice_in_dim(value, 0, width, axis=dim)
        before = lax.ppermute(last, axis, up)
        after = lax.ppermute(leading, axis, down)
        value = jnp.concatenate([before, value, after], axis=dim)
    return value


def norm_act(h, gain, shift):
    mean = jnp.sum(h, axis=-1, keepdims=True) * (1.0 / h.shape[-1])
    cen = h - mean
    var = jnp.sum(cen * cen, axis=-1, keepdims=True) * (1.0 / h.shape[-1])
    z = cen * lax.rsqrt(var + NORM_EPS) * gain + shift
    return (z * R2) * (1.0 + lax.erf(z))

def conv_kernel(xt_ref, xh_ref, w0_ref, gain_ref, shift_ref, pg_ref, ps_ref, pb_ref, wm_hbm, wl_hbm, wp_hbm,
                out_ref, a0, a1, a2, a3, a4, a5, hal, wm, wl, wp, sems):
    copies = [pltpu.make_async_copy(wm_hbm.at[i], wm.at[i], sems.at[i]) for i in range(4)]
    copies += [pltpu.make_async_copy(wl_hbm.at[i], wl.at[i], sems.at[4 + i]) for i in range(2)]
    copies += [pltpu.make_async_copy(wp_hbm, wp, sems.at[6])]
    for c in copies:
        c.start()
    f32, bf = jnp.float32, jnp.bfloat16
    dn = (((0,), (0,)), ((), ()))
    g0, s0 = gain_ref[0:1, :], shift_ref[0:1, :]
    w0 = w0_ref[...]

    def put(li, rows):
        for t in range(4):
            hal[li, t, 0:rows.shape[0], :] = rows[:, 128 * t:128 * t + 128]

    def pick(li, start, size, stride=1):
        ds = pl.ds(start, size, stride=stride) if stride > 1 else pl.ds(start, size)
        return jnp.concatenate([hal[li, t, ds, :] for t in range(4)], axis=1)
    h = lax.dot_general(xh_ref[...].astype(bf), w0, (((1,), (0,)), ((), ())), preferred_element_type=f32)
    put(0, norm_act(h, g0, s0))

    def l0(i, c):
        for q in range(2):
            p = 2 * i + q
            win = xt_ref[pl.ds(5 * p, 16), :].astype(bf)
            h = lax.dot_general(win, w0, dn, preferred_element_type=f32)
            a = norm_act(h, g0, s0).astype(bf)
            a0[p] = a[0:64]
            a0[p + 32] = a[64:128]
        return c
    lax.fori_loop(0, 16, l0, 0)

    srcs = [a0, a1, a2, a3, a4, a5]
    counts = [32, 16, 8, 4, 2, 1]
    for L in range(1, 7):
        src = srcs[L - 1]
        n = counts[L - 1]
        K = 3 if L <= 4 else 2
        copies[L - 1].wait()
        w = (lambda k, L=L: wm[L - 1, k]) if L <= 4 else (lambda k, L=L: wl[L - 5, k])
        g, s = gain_ref[L:L + 1, :], shift_ref[L:L + 1, :]
        G = min(4, n)
        if K == 3:
            up = jnp.concatenate([src[0].astype(f32)[1:64], pick(L - 1, 0, 1)], axis=0)
            src[2 * n] = up.astype(bf)
        def body(i, c, src=src, n=n, K=K, G=G, w=w, g=g, s=s, L=L, halo=False):
            acc = None
            for k in range(K):
                lhs = [src[2 * (G * i + q) + k] for q in range(G)]
                if halo:
                    lhs.append(jnp.concatenate([pick(L - 1, k, 8, 2), jnp.zeros((8, 512), f32)], axis=0).astype(bf))
                lhs = jnp.concatenate(lhs, axis=0) if len(lhs) > 1 else lhs[0]
                d = jnp.dot(lhs, w(k), preferred_element_type=f32)
                acc = d if acc is None else acc + d
            a = norm_act(acc, g, s)
            if halo:
                put(L, a[64 * G:64 * G + 8])
            if L < 6:
                dst = srcs[L]
                for q in range(G):
                    dst[G * i + q] = a[64 * q:64 * q + 64].astype(bf)
                return c
            return a
        r = body(0, 0, halo=(L <= 3))
        if n // G > 1:
            lax.fori_loop(1, n // G, body, 0)
    v = r.astype(bf).astype(f32)
    mean = jnp.sum(v, axis=-1, keepdims=True) * (1.0 / 512)
    cen = v - mean
    var = jnp.sum(cen * cen, axis=-1, keepdims=True) * (1.0 / 512)
    nf = (cen * lax.rsqrt(var + NORM_EPS) * pg_ref[...] + ps_ref[...]).astype(bf)
    copies[6].wait()
    out_ref[...] = (jnp.dot(nf, wp[...], preferred_element_type=f32) + pb_ref[...]).astype(bf)


def conv_stack_call(xt, xh, conv_first, conv_mid, conv_last, conv_gain, conv_shift, proj_gain, proj_shift, proj_weight, proj_bias):
    w0 = jnp.concatenate([conv_first, jnp.zeros((6, 512), conv_first.dtype)], axis=0)
    V = pl.BlockSpec(memory_space=pltpu.VMEM)
    A = pl.BlockSpec(memory_space=pl.ANY)
    bf = jnp.bfloat16
    return pl.pallas_call(
        conv_kernel,
        out_shape=jax.ShapeDtypeStruct((64, 1280), bf),
        in_specs=[V] * 8 + [A] * 3,
        out_specs=V,
        scratch_shapes=[pltpu.VMEM((65, 64, 512), bf), pltpu.VMEM((33, 64, 512), bf), pltpu.VMEM((17, 64, 512), bf),
                        pltpu.VMEM((9, 64, 512), bf), pltpu.VMEM((4, 64, 512), bf), pltpu.VMEM((2, 64, 512), bf),
                        pltpu.VMEM((4, 4, 24, 128), jnp.float32),
                        pltpu.VMEM((4, 3, 512, 512), bf), pltpu.VMEM((2, 2, 512, 512), bf), pltpu.VMEM((512, 1280), bf),
                        pltpu.SemaphoreType.DMA((7,))],
        compiler_params=pltpu.CompilerParams(vmem_limit_bytes=50 << 20),
        name="conv_stack",
    )(xt, xh, w0, conv_gain * R2, conv_shift * R2, proj_gain[None], proj_shift[None], proj_bias[None], conv_mid, conv_last, proj_weight)


def prep_samples(own, nxt):
    fr = own.reshape(64, 320).astype(jnp.float32)
    nx = nxt.astype(jnp.float32)
    tail = jnp.concatenate([fr[1:, :16], nx[None, :16]], axis=0)
    S = jnp.concatenate([fr, tail], axis=1)
    xt = jnp.concatenate([S[:, :176], S[:, 160:336]], axis=0).T
    idx = nx[:80].reshape(16, 5)
    nxt_idx = jnp.concatenate([idx[1:], jnp.zeros((1, 5), jnp.float32)], axis=0)
    xh = jnp.concatenate([idx, nxt_idx, jnp.zeros((16, 6), jnp.float32)], axis=1)
    return xt, xh

WROWS = 133 * 80 + 16

def pos_kernel(src_ref, wb_hbm, bias_ref, out_ref, x3, cc, wb, sems):
    f32, bf = jnp.float32, jnp.bfloat16
    copies = [pltpu.make_async_copy(wb_hbm.at[g], wb.at[g], sems.at[g]) for g in range(2)]
    for c in copies:
        c.start()
    lane = lax.broadcasted_iota(jnp.int32, (96 * 8, 128), 1)
    cc[...] = jnp.concatenate([src_ref[2, 64:128].reshape(32, 2, 8, 128)[:, 0].reshape(256, 128)] * 2, axis=1).astype(bf)
    for a in range(3):
        full = src_ref[a].reshape(97, 2, 8, 128)
        ev, od = full[:, 0].reshape(97 * 8, 128), full[:, 1].reshape(97 * 8, 128)
        for par in range(2):
            f0 = (ev if par == 0 else od)[0:768]
            f1 = od[0:768] if par == 0 else ev[8:776]
            f2 = (ev if par == 0 else od)[8:776]
            r1 = pltpu.roll(f1, 80, 1)
            r2 = pltpu.roll(f2, 32, 1)
            v0 = jnp.where(lane < 80, f0, r1)
            v1 = jnp.where(lane < 32, r1, jnp.where(lane < 112, r2, 0.0))
            v = jnp.concatenate([v0, v1], axis=1)
            x3[a, par, 0] = v.astype(bf)
            x3[a, par, 1, 0:752, :] = v[8:760].astype(bf)
    for c in copies:
        c.wait()
    plan = ((0, 0, 0), (1, 1, 0), (0, 1, 16), (1, 0, 32))

    def body(i, acc):
        ctr = cc[...]
        masks = []
        for par, al, off in plan:
            masks.append(x3[2, par, al, pl.ds(pl.multiple_of(48 * i, 16) + off, 256), :] == ctr)
        out = []
        for g in range(2):
            lhs = jnp.concatenate([
                jnp.where(m, x3[g, par, al, pl.ds(pl.multiple_of(48 * i, 16) + off, 256), :], jnp.zeros((), bf))
                for m, (par, al, off) in zip(masks, plan)], axis=1)
            rhs = jnp.concatenate([
                jnp.concatenate([wb[g, pl.ds(pl.multiple_of(960 * i, 16) + 240 * s + 80, 256), :],
                                 wb[g, pl.ds(pl.multiple_of(960 * i, 16) + 240 * s, 256), :]], axis=1)
                for s in range(4)], axis=0)
            out.append(acc[g] + jnp.dot(lhs, rhs, preferred_element_type=f32))
        return tuple(out)
    acc = lax.fori_loop(0, 11, body, (jnp.zeros((256, 256), f32),) * 2)
    for g in range(2):
        halves = []
        for v in range(2):
            pos = acc[g][:, 128 * v:128 * v + 128] + bias_ref[g]
            own = src_ref[g, 64:128].reshape(32, 2, 8, 128)[:, v].reshape(256, 128)
            cid = src_ref[2, 64:128].reshape(32, 2, 8, 128)[:, v].reshape(256, 128)
            gel = 0.5 * pos * (1.0 + lax.erf(pos * 0.7071067811865476))
            res = jnp.where(cid >= 0.0, own + gel, 0.0)
            halves.append(res.reshape(32, 1, 8, 128))
        out_ref[g] = jnp.concatenate(halves, axis=1).reshape(64, 8, 128)

def pos_call(src, wb, bias):
    V = pl.BlockSpec(memory_space=pltpu.VMEM)
    A = pl.BlockSpec(memory_space=pl.ANY)
    bf = jnp.bfloat16
    return pl.pallas_call(
        pos_kernel,
        out_shape=jax.ShapeDtypeStruct((2, 64, 8, 128), jnp.float32),
        in_specs=[V, A, V], out_specs=V,
        scratch_shapes=[pltpu.VMEM((3, 2, 2, 768, 256), bf), pltpu.VMEM((256, 256), bf), pltpu.VMEM((2, WROWS, 128), bf),
                        pltpu.SemaphoreType.DMA((2,))],
        compiler_params=pltpu.CompilerParams(vmem_limit_bytes=50 << 20),
        name="pos_conv",
    )(src, wb, bias)

def pad_weights(w):
    w = w.reshape(2, 128 * 80, 80)
    return jnp.pad(w, ((0, 0), (80, WROWS - 80 - 10240), (0, 48)))


def frame_segments(col_lengths, frame_ids):
    clip_ends = jnp.cumsum((col_lengths // 320).reshape(-1), dtype=jnp.int32)
    clip_index = jnp.sum(
        (clip_ends[None, :] <= frame_ids[:, None]).astype(jnp.int32), axis=1, dtype=jnp.int32
    )
    marker = jnp.arange(clip_ends.shape[0], dtype=jnp.int32)
    end_frame = jnp.sum(
        jnp.where(marker[None, :] == clip_index[:, None], clip_ends[None, :], 0),
        axis=1,
        dtype=jnp.int32,
    )
    usable = (frame_ids >= 0) & (frame_ids + 1 < end_frame)
    return (clip_index, usable)


def per_device(
    waveform,
    clip_lengths,
    conv_first,
    conv_mid,
    conv_last,
    conv_gain,
    conv_shift,
    proj_gain,
    proj_shift,
    proj_weight,
    proj_bias,
    pos_weight,
    pos_bias,
):
    dp_size = lax.axis_size("dp")
    fs_size = lax.axis_size("fsdp")
    my_rank = lax.axis_index("dp")
    column = lax.axis_index("fsdp")
    capacity = waveform.shape[1]
    block_len = waveform.shape[2]
    send_slots = (capacity + dp_size - 1) // dp_size
    half = TAPS // 2
    frame_rows = NB * FPB
    col_lengths = lax.dynamic_index_in_dim(clip_lengths, column, 0, keepdims=False)
    block_counts = jnp.sum(col_lengths, axis=1, dtype=jnp.int32) // block_len
    starts = jnp.cumsum(block_counts, dtype=jnp.int32) - block_counts
    sources = jnp.arange(dp_size, dtype=jnp.int32)
    my_start = starts[my_rank]
    my_blocks = waveform[0]
    tail_part = jnp.concatenate([my_blocks[1:, :128], jnp.zeros((1, 128), my_blocks.dtype)], axis=0)
    strips = jnp.concatenate([my_blocks, tail_part], axis=1)
    width = strips.shape[1]
    padded = jnp.concatenate(
        [strips, jnp.zeros((send_slots * dp_size - capacity, width), strips.dtype)], axis=0
    )
    received = lax.all_to_all(
        jnp.roll(padded.reshape(send_slots, dp_size, width), my_start % dp_size, axis=1),
        "dp",
        split_axis=1,
        concat_axis=0,
        tiled=True,
    )
    item_index = jnp.arange(send_slots, dtype=jnp.int32)
    local_pos = item_index[None, :] * dp_size + (my_rank - starts[:, None]) % dp_size
    live = local_pos < block_counts[:, None]
    target = (starts[:, None] + local_pos) // dp_size
    chooser = (
        target.reshape(-1)[None, :] == jnp.arange(NB, dtype=jnp.int32)[:, None]
    ) & live.reshape(-1)[None, :]
    flat_rows = received.reshape(dp_size * send_slots, -1)
    arrived = jnp.dot(
        chooser.astype(flat_rows.dtype), flat_rows, preferred_element_type=jnp.float32
    ).astype(flat_rows.dtype)
    slots_back = (NB + dp_size - 1) // dp_size
    item_index = jnp.arange(slots_back, dtype=jnp.int32)
    slot_ids = jnp.arange(NB, dtype=jnp.int32)

    def first_slot(target_rank, source_rank):
        return jnp.maximum((target_rank * NB - source_rank + dp_size - 1) // dp_size, 0)

    targets = jnp.arange(dp_size, dtype=jnp.int32)
    slot_index = first_slot(targets, my_rank)[:, None] + item_index[None, :]
    usable_out = (slot_index < NB) & ((my_rank + slot_index * dp_size) // NB == targets[:, None])
    picker = (slot_index.reshape(-1)[:, None] == slot_ids[None, :]) & usable_out.reshape(-1)[
        :, None
    ]
    sending = jnp.dot(
        picker.astype(arrived.dtype), arrived, preferred_element_type=jnp.float32
    ).astype(arrived.dtype)
    returned = lax.all_to_all(
        sending.reshape(dp_size, slots_back, -1), "dp", split_axis=0, concat_axis=0, tiled=True
    )
    slot_in = first_slot(my_rank, sources)[:, None] + item_index[None, :]
    usable_in = (slot_in < NB) & ((sources[:, None] + slot_in * dp_size) // NB == my_rank)
    position = sources[:, None] + slot_in * dp_size - my_rank * NB
    placer = (position.reshape(-1)[None, :] == slot_ids[:, None]) & usable_in.reshape(-1)[None, :]
    ordered = jnp.dot(
        placer.astype(returned.dtype),
        returned.reshape(dp_size * slots_back, -1),
        preferred_element_type=jnp.float32,
    ).astype(returned.dtype)
    xt, xh = prep_samples(ordered[:, :block_len], ordered[NB - 1, block_len:])
    projected = conv_stack_call(
        xt, xh, conv_first, conv_mid, conv_last, conv_gain, conv_shift, proj_gain, proj_shift, proj_weight, proj_bias
    )
    group_here = pos_weight.shape[0]
    group_width = pos_weight.shape[2]
    width_here = group_here * group_width
    mine = lax.all_to_all(
        projected.reshape(1, frame_rows, fs_size, width_here), "fsdp", split_axis=2, concat_axis=0, tiled=True
    )[:, :, 0, :]
    extended = padded_2(mine, (("dp", 1),), half)
    frame_ids = my_rank * frame_rows - half + jnp.arange(frame_rows + TAPS, dtype=jnp.int32)
    clip_ids, usables = jax.vmap(lambda col: frame_segments(col, frame_ids))(clip_lengths)
    lanes = jnp.transpose(extended, (1, 0, 2)).reshape(frame_rows + TAPS, fs_size, group_here, group_width)
    lanes = jnp.pad(lanes.transpose(2, 0, 1, 3).astype(jnp.float32), ((0, 0), (0, 2), (0, 0), (0, 48)))
    marks = jnp.where(usables, clip_ids, -1).T.astype(jnp.float32)
    marks = jnp.pad(marks, ((0, 2), (0, 0)), constant_values=-1)
    marks = jnp.broadcast_to(marks[None, :, :, None], (1, frame_rows + TAPS + 2, fs_size, 128))
    bias_part = lax.dynamic_slice_in_dim(pos_bias, column * width_here, width_here, 0)
    bias_part = jnp.pad(bias_part.reshape(group_here, 1, group_width), ((0, 0), (0, 0), (0, 48)))
    finished = pos_call(jnp.concatenate([lanes, marks], axis=0), pad_weights(pos_weight), bias_part)
    finished = finished[..., :group_width].astype(jnp.bfloat16).transpose(2, 1, 0, 3)
    answered = lax.all_to_all(
        finished.reshape(fs_size, frame_rows, 1, width_here), "fsdp", split_axis=0, concat_axis=2, tiled=True
    )
    return answered.reshape(1, frame_rows, -1)


def solution(mesh):
    return jax.shard_map(
        per_device,
        mesh=mesh,
        in_specs=(
            P("fsdp", "dp", None),
            P(),
            P(),
            P(),
            P(),
            P(),
            P(),
            P(),
            P(),
            P(),
            P(),
            P("fsdp", None, None, None),
            P(),
        ),
        out_specs=P("fsdp", "dp", None),
        check_vma=False,
    )
```

profile of v0, /device:TPU:1, one launch (start us, length us, event | category | flops | bytes accessed | tf_op | source)
XLA Modules:
  0.0 143.3 jit_solution(15436039573737730906)
XLA Ops:
  0.0 0.7 bitcast_select_fusion.1
  0.9 0.6 dynamic_slice.15
  3.5 0.7 slice.51
  4.2 0.9 fusion.3
  5.4 0.6 broadcast.639
  6.0 1.2 reduce.5
  7.2 0.8 reshape.402
  8.0 12.0 %all-to-all-start = ((bf16[32,2,704]{2,1,0:T(2,128)(2,1)}), bf16[32,2,704]{2,1,0:T(2,128)(2,1)S(1)}, u32[]{:S(2)}, u32[]{:S(2)}) async-start(bf16[32,2,704]{2,1,0:T(2,128)(2,1)} %reshape.402), calls=%async_computation | async-start | bytes 196608 | tf_op jit(solution)/shard_map/all_to_all | solution.py:268
  20.0 0.7 and_select_fusion
  21.0 0.7 broadcast_in_dim.22.pb_ref
  21.8 0.6 pad.35.clone
  22.4 0.7 concatenate.46.w0_ref
  23.2 6.0 %all-to-all-done = bf16[32,2,704]{2,1,0:T(2,128)(2,1)S(1)} async-done(((bf16[32,2,704]{2,1,0:T(2,128)(2,1)}), bf16[32,2,704]{2,1,0:T(2,128)(2,1)S(1)}, u32[]{:S(2)}, u32[]{:S(2)}) %all-to-all-start) | async-done | bytes 90144 | tf_op jit(solution)/shard_map/all_to_all | solution.py:268
  29.5 0.7 reduce.6
  30.3 0.8 reshape.404
  31.1 4.7 %all-to-all-start.1 = ((bf16[32,2,704]{2,1,0:T(2,128)(2,1)}), bf16[32,2,704]{2,1,0:T(2,128)(2,1)}, u32[]{:S(2)}, u32[]{:S(2)}) async-start(bf16[32,2,704]{2,1,0:T(2,128)(2,1)} %reshape.404), calls=%async_computation.1 | async-start | bytes 196608 | tf_op jit(solution)/shard_map/all_to_all | solution.py:302
  35.8 0.7 broadcast_multiply_fusion
  36.5 8.5 %all-to-all-done.1 = bf16[32,2,704]{2,1,0:T(2,128)(2,1)} async-done(((bf16[32,2,704]{2,1,0:T(2,128)(2,1)}), bf16[32,2,704]{2,1,0:T(2,128)(2,1)}, u32[]{:S(2)}, u32[]{:S(2)}) %all-to-all-start.1) | async-done | bytes 90144 | tf_op jit(solution)/shard_map/all_to_all | solution.py:302
  45.0 1.7 %reshape.405 = bf16[32,1,1408]{2,1,0:T(2,128)(2,1)} reshape(bf16[32,2,704]{2,1,0:T(2,128)(2,1)} %all-to-all-done.1) | data formatting | bytes 180224
  46.7 1.2 convolution_convert_fusion
  47.9 0.9 slice_convert_fusion.1
  48.9 1.9 %copy.92 = f32[16,1280]{1,0:T(8,128)} copy(f32[16,1280]{0,1:T(8,128)} %slice_convert_fusion.1) | data formatting | bytes 163840 | tf_op jit(solution)/shard_map/convert_element_type | solution.py:133
  50.8 1.6 %reshape.398 = f32[64,320]{1,0:T(8,128)} reshape(f32[16,1280]{1,0:T(8,128)} %copy.92) | data formatting | bytes 163840 | tf_op jit(solution)/shard_map/convert_element_type | solution.py:133
  52.4 1.7 %copy.93 = f32[64,320]{0,1:T(8,128)} copy(f32[64,320]{1,0:T(8,128)} %reshape.398) | data formatting | bytes 163840 | tf_op jit(solution)/shard_map/convert_element_type | solution.py:133
  54.1 1.4 slice.54
  55.5 1.5 %slice.53 = f32[64,176]{0,1:T(8,128)} slice(f32[64,320]{0,1:T(8,128)} %copy.93), slice={[0:64], [0:176]} | slice | bytes 90112 | tf_op jit(solution)/shard_map/slice | solution.py:137
  57.0 0.6 slice.56
  57.6 0.6 slice_reduce_fusion
  58.2 0.7 slice_reduce_fusion.1
  58.9 0.7 slice.49
  59.6 0.8 reshape.392
  60.3 1.1 fusion.6.xt_ref
  61.4 0.7 fusion.15.xh_ref
  62.1 22.1 %conv_stack.1 = bf16[64,1280]{1,0:T(8,128)(2,1)S(1)} custom-call(f32[176,128]{1,0:T(8,128)S(1)} %fusion.6.xt_ref, f32[16,16]{1,0:T(8,128)S(1)} %fusion.15.xh_ref, bf16[16,512]{1,0:T(8,128)(2,1)S(1)} %concatenate.46.w0_ref, f32[7,512]{1,0:T(8,128)S(1)} %get-tuple-element.16.gain_ref, f32[7,512]{1,0:T(8,128)S(1)} %get-tuple-element.15.shift_ref, ...), custom_call_target="tpu_custom_call" | custom-call | tf_op jit(solution)/shard_map/conv_stack/pallas_call | solution.py:117
  84.3 0.7 copy-done.2
  84.9 1.3 reshape.393
  86.2 0.7 copy.96
  86.9 7.4 %all-to-all-start.2 = ((bf16[1,64,8,160]{3,1,0,2:T(8,128)(2,1)}), bf16[1,64,8,160]{3,1,0,2:T(8,128)(2,1)S(1)}, u32[]{:S(2)}, u32[]{:S(2)}) async-start(bf16[1,64,8,160]{3,1,0,2:T(8,128)(2,1)} %copy.96), calls=%async_computation.2 | async-start | bytes 524288 | tf_op jit(solution)/shard_map/all_to_all | solution.py:321
  94.5 6.3 %all-to-all-done.2 = bf16[1,64,8,160]{3,1,0,2:T(8,128)(2,1)S(1)} async-done(((bf16[1,64,8,160]{3,1,0,2:T(8,128)(2,1)}), bf16[1,64,8,160]{3,1,0,2:T(8,128)(2,1)S(1)}, u32[]{:S(2)}, u32[]{:S(2)}) %all-to-all-start.2) | async-done | bytes 163872 | tf_op jit(solution)/shard_map/all_to_all | solution.py:321
  101.0 1.3 collective-permute-start.1
  102.3 4.2 %collective-permute-start = (bf16[8,64,160]{1,2,0:T(8,128)(2,1)S(1)}, bf16[8,64,160]{1,2,0:T(8,128)(2,1)S(1)}, u32[]{:S(2)}, u32[]{:S(2)}) collective-permute-start(bf16[8,64,160]{1,2,0:T(8,128)(2,1)S(1)} %bitcast.68), channel_id=1, source_target_pairs={{0,8},{8,16},{16,24},{24,32},{32,40},{40,48},{48,56},{56,64},{64,7... | collective-permute-start | bytes 491528 | tf_op jit(solution)/shard_map/ppermute | solution.py:23
  106.6 7.9 %copy.100 = bf16[2,128,80,80]{3,2,1,0:T(8,128)(2,1)} copy(bf16[2,128,80,80]{1,3,2,0:T(8,128)(2,1)} %param.24) | data formatting | bytes 6553600 | tf_op args[11]
  114.6 6.2 %pad.26.wb_hbm = bf16[2,10656,128]{2,1,0:T(8,128)(2,1)} pad(bf16[2,10240,80]{2,1,0:T(8,128)(2,1)} %bitcast.64, bf16[]{:T(256)} %constant.144.clone.1), padding=0_0x80_336x0_48 | pad | bytes 8732674 | tf_op jit(solution)/shard_map/jit(_pad)/pad | solution.py:214
  120.8 0.8 dynamic_slice.17
  122.0 0.4 copy.98
  123.0 8.3 %pos_conv.1 = f32[2,64,8,128]{3,2,1,0:T(8,128)S(1)} custom-call(f32[3,194,8,128]{3,2,1,0:T(8,128)S(1)} %pad_maximum_fusion.src_ref, bf16[2,10656,128]{2,1,0:T(8,128)(2,1)} %pad.26.wb_hbm, f32[2,1,128]{2,1,0:T(1,128)S(1)} %pad.27.bias_ref), custom_call_target="tpu_custom_call" | custom-call | tf_op jit(solution)/shard_map/pos_conv/pallas_call | solution.py:202
  131.8 10.5 %all_to_all.44 = bf16[8,64,1,160]{3,1,2,0:T(8,128)(2,1)S(1)} all-to-all(bf16[8,64,1,160]{3,1,2,0:T(8,128)(2,1)S(1)} %bitcast.70), channel_id=1, replica_groups=mesh['dp'=32,'fsdp'=8] {'fsdp'}, dimensions={0} | all-to-all | bytes 327680 | tf_op jit(solution)/shard_map/all_to_all | solution.py:336
  142.4 0.9 reshape.397
  (45 shorter events, 3.4 us)
Async XLA Ops:
  8.0 21.2 %all-to-all-start = ((bf16[32,2,704]{2,1,0:T(2,128)(2,1)}), bf16[32,2,704]{2,1,0:T(2,128)(2,1)S(1)}, u32[]{:S(2)}, u32[]{:S(2)}) async-start(bf16[32,2,704]{2,1,0:T(2,128)(2,1)} %reshape.402), calls=%async_computation | async-start | bytes 196608 | tf_op jit(solution)/shard_map/all_to_all | solution.py:268
  30.2 31.8 %copy-start = (bf16[2,2,512,512]{3,2,1,0:T(8,128)(2,1)S(1)}, bf16[2,2,512,512]{3,2,1,0:T(8,128)(2,1)}, u32[]{:S(2)}) copy-start(bf16[2,2,512,512]{3,2,1,0:T(8,128)(2,1)} %wl_hbm.1) | copy-start | bytes 6291460
  30.3 31.8 %copy-start.1 = (bf16[512,1280]{1,0:T(8,128)(2,1)S(1)}, bf16[512,1280]{1,0:T(8,128)(2,1)}, u32[]{:S(2)}) copy-start(bf16[512,1280]{1,0:T(8,128)(2,1)} %wp_hbm.1) | copy-start | bytes 3932164
  30.3 31.8 %copy-start.3 = (f32[512]{0:T(512)S(1)}, f32[512]{0:T(512)}, u32[]{:S(2)}) copy-start(f32[512]{0:T(512)} %param.20) | copy-start | bytes 6148
  30.3 31.8 %copy-start.4 = (f32[512]{0:T(512)S(1)}, f32[512]{0:T(512)}, u32[]{:S(2)}) copy-start(f32[512]{0:T(512)} %param.21) | copy-start | bytes 6148
  31.1 13.9 %all-to-all-start.1 = ((bf16[32,2,704]{2,1,0:T(2,128)(2,1)}), bf16[32,2,704]{2,1,0:T(2,128)(2,1)}, u32[]{:S(2)}, u32[]{:S(2)}) async-start(bf16[32,2,704]{2,1,0:T(2,128)(2,1)} %reshape.404), calls=%async_computation.1 | async-start | bytes 196608 | tf_op jit(solution)/shard_map/all_to_all | solution.py:302
  84.3 0.7 copy-start.2
  86.9 13.9 %all-to-all-start.2 = ((bf16[1,64,8,160]{3,1,0,2:T(8,128)(2,1)}), bf16[1,64,8,160]{3,1,0,2:T(8,128)(2,1)S(1)}, u32[]{:S(2)}, u32[]{:S(2)}) async-start(bf16[1,64,8,160]{3,1,0,2:T(8,128)(2,1)} %copy.96), calls=%async_computation.2 | async-start | bytes 524288 | tf_op jit(solution)/shard_map/all_to_all | solution.py:321
  101.0 20.6 %collective-permute-start.1 = (bf16[8,64,160]{1,2,0:T(8,128)(2,1)S(1)}, bf16[8,64,160]{1,2,0:T(8,128)(2,1)S(1)}, u32[]{:S(2)}, u32[]{:S(2)}) collective-permute-start(bf16[8,64,160]{1,2,0:T(8,128)(2,1)S(1)} %bitcast.67), channel_id=1, source_target_pairs={{8,0},{16,8},{24,16},{32,24},{40,32},{48,40},{56,48},{64,56},{72,6... | collective-permute-start | bytes 491528 | tf_op jit(solution)/shard_map/ppermute | solution.py:24
  102.3 19.3 %collective-permute-start = (bf16[8,64,160]{1,2,0:T(8,128)(2,1)S(1)}, bf16[8,64,160]{1,2,0:T(8,128)(2,1)S(1)}, u32[]{:S(2)}, u32[]{:S(2)}) collective-permute-start(bf16[8,64,160]{1,2,0:T(8,128)(2,1)S(1)} %bitcast.68), channel_id=1, source_target_pairs={{0,8},{8,16},{16,24},{24,32},{32,40},{40,48},{48,56},{56,64},{64,7... | collective-permute-start | bytes 491528 | tf_op jit(solution)/shard_map/ppermute | solution.py:23
where the time goes:
time: 145 us; the launch traced here: 143 us
  local copies, waits for them, and re-layouts  39.2 us (27%)
  Pallas kernels  30.5 us (21%)
  starting transfers between devices  29.6 us (20%)
  waiting for transfers between devices  20.8 us (14%)
  blocking collectives  10.5 us (7%)
  other arithmetic  9.01 us (6%)
  between operations  2.31 us (2%)
  matrix products  1.49 us (1%)
    pallas_call x1, Pallas kernels, conv_stack_call(): pl.pallas_call(conv_kernel, out_shape=jax.ShapeDtypeStruct((64, 1280), bf...  22.1 us
    unnamed x17, local copies, waits for them, and re-layouts  12.7 us
    all_to_all x1, starting transfers between devices, per_device(): lax.all_to_all(jnp.roll(padded.reshape(send_slots, dp_size, width), my_st...  12 us
    all_to_all x1, blocking collectives, per_device(): lax.all_to_all(finished.reshape(fs_size, frame_rows, 1, width_here), 'fsd...  10.5 us
    all_to_all x1, waiting for transfers between devices, per_device(): lax.all_to_all(sending.reshape(dp_size, slots_back, -1), 'dp', split_axis...  8.47 us
    pallas_call x1, Pallas kernels, pos_call(): pl.pallas_call(pos_kernel, out_shape=jax.ShapeDtypeStruct((2, 64, 8, 128)...  8.33 us
    all_to_all x1, starting transfers between devices, per_device(): lax.all_to_all(projected.reshape(1, frame_rows, fs_size, width_here), 'fs...  7.42 us
    all_to_all x1, waiting for transfers between devices, per_device(): lax.all_to_all(projected.reshape(1, frame_rows, fs_size, width_here), 'fs...  6.34 us
  transfers between devices with their start and end apart: 5, of which 3 were waited for; matrix products, arithmetic and copies ran while one was open for 13% of the time, Pallas kernels for 0%

commit v1 on v0

v1 whole, which is shorter than its diff:
```python
import jax
import jax.numpy as jnp
from jax import lax
from jax.experimental import pallas as pl
from jax.experimental.pallas import tpu as pltpu
from jax.sharding import PartitionSpec as P

NORM_EPS = 1e-5
R2 = 0.7071067811865476
F32, BF = jnp.float32, jnp.bfloat16
MESH = pl.DeviceIdType.MESH
NDP, NFS = 32, 8


def norm_act(h, gain, shift):
    mean = jnp.sum(h, axis=-1, keepdims=True) * (1.0 / h.shape[-1])
    cen = h - mean
    var = jnp.sum(cen * cen, axis=-1, keepdims=True) * (1.0 / h.shape[-1])
    z = cen * lax.rsqrt(var + NORM_EPS) * gain + shift
    return (z * R2) * (1.0 + lax.erf(z))


def encode_kernel(lens_ref, wave_ref, w0_ref, gain_ref, shift_ref, pg_ref, ps_ref, pb_ref, wm_hbm, wl_hbm, wp_hbm,
                  out_ref, blk, blkb, send1, recv1, send2, recv2, rows, xt, a0, a1, a2, a3, a4, a5, hal, fr, wm, wl, wp,
                  wsem, s1, r1, s2, r2):
    me, col = lax.axis_index("dp"), lax.axis_index("fsdp")
    barrier = pltpu.get_barrier_semaphore()
    for n in range(1, NDP):
        pl.semaphore_signal(barrier, inc=1, device_id={"dp": lax.rem(me + n, NDP)}, device_id_type=MESH)
    copies = [pltpu.make_async_copy(wm_hbm.at[i], wm.at[i], wsem.at[i]) for i in range(4)]
    copies += [pltpu.make_async_copy(wl_hbm.at[i], wl.at[i], wsem.at[4 + i]) for i in range(2)]
    copies += [pltpu.make_async_copy(wp_hbm, wp, wsem.at[6])]
    for c in copies:
        c.start()

    blk[...] = jnp.zeros((512, 128), F32)
    wave = wave_ref[0].astype(F32)
    for r in range(10):
        blk[pl.ds(r, 30, stride=16), :] = wave[:, 128 * r:128 * r + 128]
    blk[pl.ds(10, 29, stride=16), :] = wave[1:30, 0:128]
    blkb[...] = blk[...].astype(BF).reshape(32, 16, 128)

    def tally(s, carry):
        total, mine, owners = carry[0], carry[1], carry[2:]
        mine = jnp.where(s == me, total, mine)
        total = total + lens_ref[col, s]
        owners = tuple(o + jnp.where(total <= (me + NDP * j) * 1280, 1, 0) for j, o in enumerate(owners))
        return (total, mine) + owners
    zero = jnp.int32(0)
    res = lax.fori_loop(0, NDP, tally, (zero,) * 18)
    start, owners = res[1] // 1280, res[2:]

    for t in range(NDP):
        send1[t] = blkb[(t - start) & 31]
    recv1[me] = send1[me]
    pl.semaphore_wait(barrier, NDP - 1)
    first = []
    for n in range(1, NDP):
        to = lax.rem(me + n, NDP)
        c = pltpu.make_async_remote_copy(src_ref=send1.at[to], dst_ref=recv1.at[me], send_sem=s1.at[n],
                                         recv_sem=r1.at[n], device_id={"dp": to}, device_id_type=MESH)
        c.start()
        first.append(c)
    for c in first:
        c.wait()
    half, slot = me // 16, me % 16
    for j in range(16):
        send2[j] = recv1[jnp.minimum(owners[j], 31)]
    second = []
    for j in range(16):
        to = 2 * j + half
        c = pltpu.make_async_remote_copy(src_ref=send2.at[j], dst_ref=recv2.at[slot], send_sem=s2.at[j],
                                         recv_sem=r2.at[slot], device_id={"dp": to}, device_id_type=MESH)
        second.append((to, c))

        @pl.when(to != me)
        def _():
            c.start()

        @pl.when(to == me)
        def _():
            recv2[slot] = send2[j]
    odd = me % 2
    for i in range(16):
        c = pltpu.make_async_remote_copy(src_ref=send2.at[0], dst_ref=recv2.at[i], send_sem=s2.at[0],
                                         recv_sem=r2.at[i], device_id={"dp": me}, device_id_type=MESH)

        @pl.when(16 * odd + i != me)
        def _():
            c.wait_recv()
    for to, c in second:
        @pl.when(to != me)
        def _():
            c.wait_send()

    rows[...] = recv2[...].astype(F32).reshape(256, 128)
    flat = jnp.concatenate([rows[pl.ds(r, 16, stride=16), :] for r in range(11)], axis=1)
    y = jnp.concatenate([flat[:, 160 * e:160 * e + 256] for e in range(8)], axis=0)
    xt[...] = y.T
    halo = jnp.broadcast_to(rows[250:251, :], (16, 128))
    line = lax.broadcasted_iota(jnp.int32, (16, 128), 0)
    xh = halo
    for p in range(1, 15):
        xh = jnp.where(line == p, pltpu.roll(halo, 128 - 5 * p, 1), xh)

    dn = (((0,), (0,)), ((), ()))
    g0, b0 = gain_ref[0:1, :], shift_ref[0:1, :]
    w0 = w0_ref[...]

    def put(li, v):
        for t in range(4):
            hal[li, t, 0:v.shape[0], :] = v[:, 128 * t:128 * t + 128]

    def pick(li, begin, size, stride=1):
        ds = pl.ds(begin, size, stride=stride) if stride > 1 else pl.ds(begin, size)
        return jnp.concatenate([hal[li, t, ds, :] for t in range(4)], axis=1)

    h = jnp.dot(xh[:, 0:16].astype(BF), w0, preferred_element_type=F32)
    hal[...] = jnp.zeros(hal.shape, F32)
    put(0, norm_act(h, g0, b0))

    def l0(i, c):
        for q in range(2):
            p = 2 * i + q
            win = xt[pl.ds(5 * p, 16), :].astype(BF)
            h = lax.dot_general(win, w0, dn, preferred_element_type=F32)
            a = norm_act(h, g0, b0).astype(BF).reshape(4, 2, 16, 512)
            a0[p] = a[:, 0].reshape(64, 512)
            a0[p + 32] = a[:, 1].reshape(64, 512)
        return c
    lax.fori_loop(0, 16, l0, 0)

    srcs = [a0, a1, a2, a3, a4, a5]
    counts = [32, 16, 8, 4, 2, 1]
    for L in range(1, 7):
        src, n = srcs[L - 1], counts[L - 1]
        K = 3 if L <= 4 else 2
        G = min(4, n)
        copies[L - 1].wait()
        w = (lambda k, L=L: wm[L - 1, k]) if L <= 4 else (lambda k, L=L: wl[L - 5, k])
        g, s = gain_ref[L:L + 1, :], shift_ref[L:L + 1, :]
        if K == 3:
            v = src[0].astype(F32)
            src[2 * n] = jnp.concatenate([v[16:64], v[1:16], pick(L - 1, 0, 1)], axis=0).astype(BF)

        def body(i, c, src=src, K=K, G=G, w=w, g=g, s=s, L=L, halo=False):
            acc = None
            for k in range(K):
                lhs = [src[2 * (G * i + q) + k] for q in range(G)]
                if halo:
                    lhs.append(jnp.concatenate([pick(L - 1, k, 8, 2), jnp.zeros((8, 512), F32)], axis=0).astype(BF))
                lhs = jnp.concatenate(lhs, axis=0) if len(lhs) > 1 else lhs[0]
                d = jnp.dot(lhs, w(k), preferred_element_type=F32)
                acc = d if acc is None else acc + d
            a = norm_act(acc, g, s)
            if halo:
                put(L, a[64 * G:64 * G + 8])
            if L == 6:
                return a
            for q in range(G):
                srcs[L][G * i + q] = a[64 * q:64 * q + 64].astype(BF)
            return c
        last = body(0, 0, halo=(L <= 3))
        if n // G > 1:
            lax.fori_loop(1, n // G, body, 0)

    v = last.astype(BF).astype(F32)
    for t in range(4):
        for q in range(4):
            fr[t, pl.ds(q, 16, stride=4), :] = v[16 * q:16 * q + 16, 128 * t:128 * t + 128]
    v = jnp.concatenate([fr[t] for t in range(4)], axis=1)
    mean = jnp.sum(v, axis=-1, keepdims=True) * (1.0 / 512)
    cen = v - mean
    var = jnp.sum(cen * cen, axis=-1, keepdims=True) * (1.0 / 512)
    nf = (cen * lax.rsqrt(var + NORM_EPS) * pg_ref[...] + ps_ref[...]).astype(BF)
    copies[6].wait()
    pr = jnp.dot(nf, wp[...], preferred_element_type=F32) + pb_ref[...]
    gap = jnp.zeros((64, 48), F32)
    for q in range(8):
        parts = []
        for g in range(2):
            parts += [pr[:, 160 * q + 80 * g:160 * q + 80 * g + 80], gap]
        out_ref[q] = jnp.concatenate(parts, axis=1).astype(BF)


def encode_call(waveform, clip_lengths, conv_first, conv_mid, conv_last, conv_gain, conv_shift, proj_gain, proj_shift, proj_weight, proj_bias):
    w0 = jnp.concatenate([conv_first, jnp.zeros((6, 512), conv_first.dtype)], axis=0)
    V = pl.BlockSpec(memory_space=pltpu.VMEM)
    A = pl.BlockSpec(memory_space=pl.ANY)
    S = pl.BlockSpec(memory_space=pltpu.SMEM)
    D = pltpu.SemaphoreType.DMA
    return pl.pallas_call(
        encode_kernel,
        out_shape=jax.ShapeDtypeStruct((8, 64, 256), BF),
        in_specs=[S] + [V] * 7 + [A] * 3,
        out_specs=V,
        scratch_shapes=[pltpu.VMEM((512, 128), F32), pltpu.VMEM((32, 16, 128), BF), pltpu.VMEM((32, 16, 128), BF),
                        pltpu.VMEM((32, 16, 128), BF), pltpu.VMEM((16, 16, 128), BF), pltpu.VMEM((16, 16, 128), BF),
                        pltpu.VMEM((256, 128), F32), pltpu.VMEM((256, 128), F32),
                        pltpu.VMEM((65, 64, 512), BF), pltpu.VMEM((33, 64, 512), BF), pltpu.VMEM((17, 64, 512), BF),
                        pltpu.VMEM((9, 64, 512), BF), pltpu.VMEM((4, 64, 512), BF), pltpu.VMEM((2, 64, 512), BF),
                        pltpu.VMEM((4, 4, 24, 128), F32), pltpu.VMEM((4, 64, 128), F32),
                        pltpu.VMEM((4, 3, 512, 512), BF), pltpu.VMEM((2, 2, 512, 512), BF), pltpu.VMEM((512, 1280), BF),
                        D((7,)), D((32,)), D((32,)), D((16,)), D((16,))],
        compiler_params=pltpu.CompilerParams(vmem_limit_bytes=50 << 20, collective_id=0, has_side_effects=True),
        name="route_and_encode",
    )(clip_lengths[:, :, 0], waveform, w0, conv_gain * R2, conv_shift * R2, proj_gain[None], proj_shift[None], proj_bias[None], conv_mid, conv_last, proj_weight)


WROWS = 133 * 80 + 16
PLAN = ((0, 0, 0), (1, 1, 0), (0, 1, 16), (1, 0, 32))


def pos_kernel(slab_ref, lens_ref, bias_ref, wb_hbm, out_ref, rcv, src, x3, cc, wb, res, fin, ret, wsem, s1, r1, s2, r2):
    me, col = lax.axis_index("dp"), lax.axis_index("fsdp")
    barrier = pltpu.get_barrier_semaphore()
    peers = [(dr, dq) for dr in (0, 1, -1) for dq in range(NFS) if (dr, dq) != (0, 0)]

    def at(dr, dq):
        return {"dp": lax.rem(me + dr + NDP, NDP), "fsdp": lax.rem(col + dq + NFS, NFS)}
    for dr, dq in peers:
        pl.semaphore_signal(barrier, inc=1, device_id=at(dr, dq), device_id_type=MESH)
    weights = [pltpu.make_async_copy(wb_hbm.at[g], wb.at[g], wsem.at[g]) for g in range(2)]
    for c in weights:
        c.start()
    rcv[1, col] = slab_ref[col]
    pl.semaphore_wait(barrier, len(peers))
    sends = []
    for n, (dr, dq) in enumerate(peers):
        to = at(dr, dq)
        c = pltpu.make_async_remote_copy(src_ref=slab_ref.at[to["fsdp"]], dst_ref=rcv.at[1 - dr, col],
                                         send_sem=s1.at[n], recv_sem=r1.at[n], device_id=to, device_id_type=MESH)
        c.start()
        sends.append(c)

    row = lax.broadcasted_iota(jnp.int32, (128, 128), 0)
    lane = lax.broadcasted_iota(jnp.int32, (128, 128), 1)
    upper = jnp.where(row <= lane, 1.0, 0.0).astype(BF)
    ends = jnp.dot(lens_ref[...].astype(BF), upper, preferred_element_type=F32)
    ends = jnp.where(lax.broadcasted_iota(jnp.int32, (8, 128), 1) < NDP, ends, 1e9)
    frame = lax.broadcasted_iota(jnp.int32, (195, 8, 128), 0) + (64 * me - 64)
    past = jnp.where(ends[None] <= frame.astype(F32), 1.0, 0.0)
    clip = jnp.sum(past, axis=2, keepdims=True)
    here, after = clip[0:194], clip[1:195]
    ok = (here == after) & (frame[0:194, :, 0:1] >= 0) & (here < NDP)
    src[2, 0:1552, :] = jnp.broadcast_to(jnp.where(ok, here, -1.0), (194, 8, 128)).reshape(1552, 128)
    for c in sends:
        c.wait()

    for g in range(2):
        src[g, 1536:1552, :] = jnp.zeros((16, 128), F32)
        for part in range(3):
            for c in range(NFS):
                src[g, pl.ds(512 * part + c, 64, stride=8), :] = rcv[part, c, :, 128 * g:128 * g + 128].astype(F32)
    cc[...] = jnp.concatenate([src[2, 512:1024].reshape(32, 2, 8, 128)[:, 0].reshape(256, 128)] * 2, axis=1).astype(BF)
    lane = lax.broadcasted_iota(jnp.int32, (768, 128), 1)
    for a in range(3):
        full = src[a].reshape(97, 2, 8, 128)
        ev, od = full[:, 0].reshape(776, 128), full[:, 1].reshape(776, 128)
        for par in range(2):
            f0 = (ev if par == 0 else od)[0:768]
            f1 = od[0:768] if par == 0 else ev[8:776]
            f2 = (ev if par == 0 else od)[8:776]
            t1 = pltpu.roll(f1, 80, 1)
            t2 = pltpu.roll(f2, 32, 1)
            v0 = jnp.where(lane < 80, f0, t1)
            v1 = jnp.where(lane < 32, t1, jnp.where(lane < 112, t2, 0.0))
            v = jnp.concatenate([v0, v1], axis=1)
            x3[a, par, 0] = v.astype(BF)
            x3[a, par, 1, 0:752, :] = v[8:760].astype(BF)
    for c in weights:
        c.wait()

    def body(i, acc):
        ctr = cc[...]
        at_row = pl.multiple_of(48 * i, 16)
        tap = pl.multiple_of(960 * i, 16)
        masks = [x3[2, par, al, pl.ds(at_row + off, 256), :] == ctr for par, al, off in PLAN]
        out = []
        for g in range(2):
            lhs = jnp.concatenate([
                jnp.where(m, x3[g, par, al, pl.ds(at_row + off, 256), :], jnp.zeros((), BF))
                for m, (par, al, off) in zip(masks, PLAN)], axis=1)
            rhs = jnp.concatenate([
                jnp.concatenate([wb[g, pl.ds(tap + 240 * s + 80, 256), :], wb[g, pl.ds(tap + 240 * s, 256), :]], axis=1)
                for s in range(4)], axis=0)
            out.append(acc[g] + jnp.dot(lhs, rhs, preferred_element_type=F32))
        return tuple(out)
    acc = lax.fori_loop(0, 11, body, (jnp.zeros((256, 256), F32),) * 2)

    for g in range(2):
        halves = []
        for v in range(2):
            pos = acc[g][:, 128 * v:128 * v + 128] + bias_ref[g]
            own = src[g, 512:1024].reshape(32, 2, 8, 128)[:, v].reshape(256, 128)
            mark = src[2, 512:1024].reshape(32, 2, 8, 128)[:, v].reshape(256, 128)
            gel = 0.5 * pos * (1.0 + lax.erf(pos * R2))
            halves.append(jnp.where(mark >= 0.0, own + gel, 0.0).reshape(32, 1, 8, 128))
        res[g] = jnp.concatenate(halves, axis=1).reshape(512, 128)
        for c in range(NFS):
            fin[c, :, 128 * g:128 * g + 128] = res[g, pl.ds(c, 64, stride=8), :].astype(BF)
    ret[col] = fin[col]
    back = []
    for dq in range(1, NFS):
        to = at(0, dq)
        c = pltpu.make_async_remote_copy(src_ref=fin.at[to["fsdp"]], dst_ref=ret.at[col], send_sem=s2.at[dq],
                                         recv_sem=r2.at[dq], device_id=to, device_id_type=MESH)
        c.start()
        back.append(c)
    for c in back:
        c.wait()
    out_ref[0] = jnp.concatenate(
        [ret[q, :, 128 * g:128 * g + 80] for q in range(NFS) for g in range(2)], axis=1)


def pos_call(slabs, clip_lengths, pos_weight, bias):
    V = pl.BlockSpec(memory_space=pltpu.VMEM)
    A = pl.BlockSpec(memory_space=pl.ANY)
    D = pltpu.SemaphoreType.DMA
    lens = jnp.pad((clip_lengths[:, :, 0] // 320).astype(F32), ((0, 0), (0, 128 - NDP)))
    w = pos_weight.reshape(2, 128 * 80, 80)
    wb = jnp.pad(w, ((0, 0), (80, WROWS - 80 - 10240), (0, 48)))
    return pl.pallas_call(
        pos_kernel,
        out_shape=jax.ShapeDtypeStruct((1, 64, 1280), BF),
        in_specs=[V, V, V, A], out_specs=V,
        scratch_shapes=[pltpu.VMEM((3, 8, 64, 256), BF), pltpu.VMEM((3, 1552, 128), F32), pltpu.VMEM((3, 2, 2, 768, 256), BF),
                        pltpu.VMEM((256, 256), BF), pltpu.VMEM((2, WROWS, 128), BF), pltpu.VMEM((2, 512, 128), F32),
                        pltpu.VMEM((8, 64, 256), BF), pltpu.VMEM((8, 64, 256), BF),
                        D((2,)), D((23,)), D((23,)), D((8,)), D((8,))],
        compiler_params=pltpu.CompilerParams(vmem_limit_bytes=50 << 20, collective_id=1, has_side_effects=True),
        name="positional_conv",
    )(slabs, lens, bias, wb)


def per_device(waveform, clip_lengths, conv_first, conv_mid, conv_last, conv_gain, conv_shift, proj_gain, proj_shift,
               proj_weight, proj_bias, pos_weight, pos_bias):
    column = lax.axis_index("fsdp")
    slabs = encode_call(waveform, clip_lengths, conv_first, conv_mid, conv_last, conv_gain, conv_shift, proj_gain,
                        proj_shift, proj_weight, proj_bias)
    bias = lax.dynamic_slice_in_dim(pos_bias, column * 160, 160, 0)
    bias = jnp.pad(bias.reshape(2, 1, 80), ((0, 0), (0, 0), (0, 48)))
    return pos_call(slabs, clip_lengths, pos_weight, bias)


def solution(mesh):
    return jax.shard_map(
        per_device,
        mesh=mesh,
        in_specs=(P("fsdp", "dp", None),) + (P(),) * 10 + (P("fsdp", None, None, None), P()),
        out_specs=P("fsdp", "dp", None),
        check_vma=False,
    )
```

time: 145 us -> 99.2 us (0.68)
  Pallas kernels: 30.5 us -> 75.2 us
  starting transfers between devices: 29.6 us -> 0 us
  waiting for transfers between devices: 20.8 us -> 0 us
  local copies, waits for them, and re-layouts: 39.2 us -> 21.9 us
  blocking collectives: 10.5 us -> 0 us
  other arithmetic: 9.01 us -> 1.44 us
  between operations: 2.31 us -> 0.04 us
  matrix products: 1.49 us -> 0 us
    pallas_call x2, Pallas kernels: 30.5 us -> 75.2 us  [the longest x1 43.1 us: encode_call(): pl.pallas_call(encode_kernel, out_shape=jax.ShapeDtypeStruct((8, 64, 256)...]
    all_to_all x3 -> x0, starting transfers between devices: 24.1 us -> none  [the longest x1 12 us: per_device(): lax.all_to_all(jnp.roll(padded.reshape(send_slots, dp_size, width), my_st...]
    all_to_all x3 -> x0, waiting for transfers between devices: 20.8 us -> none  [the longest x1 8.47 us: per_device(): lax.all_to_all(sending.reshape(dp_size, slots_back, -1), 'dp', split_axis...]
    all_to_all x1 -> x0, blocking collectives: 10.5 us -> none  [per_device(): lax.all_to_all(finished.reshape(fs_size, frame_rows, 1, width_here), 'fsd...]
    slice x7 -> x0, local copies, waits for them, and re-layouts: 6.17 us -> none  [the longest x2 1.97 us: prep_samples(): tail = jnp.concatenate([fr[1:, :16], nx[None, :16]], axis=0)]
    convert_element_type x4 -> x0, local copies, waits for them, and re-layouts: 5.63 us -> none  [the longest x3 5.2 us: prep_samples(): fr = own.reshape(64, 320).astype(jnp.float32)]
    ppermute x2 -> x0, starting transfers between devices: 5.48 us -> none  [the longest x1 4.19 us: padded_2(): before = lax.ppermute(last, axis, up)]
    reshape x7 -> x1, local copies, waits for them, and re-layouts: 3.92 us -> 0.08 us  [per_device(): bias = jnp.pad(bias.reshape(2, 1, 80), ((0, 0), (0, 0), (0, 48)))]
  transfers between devices with their start and end apart: 5 -> 0, of which waited for: 3 -> 0; matrix products, arithmetic and copies ran while one was open for 13% -> 0% of each run, Pallas kernels for 0% -> 0%
where the time goes in v1:
time: 99.2 us; the launch traced here: 98.6 us
  Pallas kernels  75.2 us (76%)
  local copies, waits for them, and re-layouts  21.9 us (22%)
  other arithmetic  1.44 us (1%)
    pallas_call x1, Pallas kernels, encode_call(): pl.pallas_call(encode_kernel, out_shape=jax.ShapeDtypeStruct((8, 64, 256)...  43.1 us
    pallas_call x1, Pallas kernels, pos_call(): pl.pallas_call(pos_kernel, out_shape=jax.ShapeDtypeStruct((1, 64, 1280),...  32.1 us
    unnamed x16, local copies, waits for them, and re-layouts  13.4 us
    pad x1, local copies, waits for them, and re-layouts, pos_call(): wb = jnp.pad(w, ((0, 0), (80, WROWS - 80 - 10240), (0, 48)))  6.18 us

profile of v1, /device:TPU:1, one launch (start us, length us, event | category | flops | bytes accessed | tf_op | source)
XLA Modules:
  0.0 98.6 jit_solution(9441428218868899120)
XLA Ops:
  0.0 0.8 dynamic_slice.3
  0.8 0.1 reshape.6
  0.9 0.7 fusion
  1.6 0.7 broadcast_in_dim.12.pb_ref
  2.3 0.7 concatenate.3.w0_ref
  3.0 0.7 broadcast_multiply_fusion
  3.7 0.0 copy-start
  3.7 1.6 %copy-done = bf16[2,2,512,512]{3,2,1,0:T(8,128)(2,1)S(1)} copy-done((bf16[2,2,512,512]{3,2,1,0:T(8,128)(2,1)S(1)}, bf16[2,2,512,512]{3,2,1,0:T(8,128)(2,1)}, u32[]{:S(2)}) %copy-start) | copy-done | bytes 2097176
  5.3 0.0 copy-start.1
  5.3 1.3 %copy-done.1 = bf16[512,1280]{1,0:T(8,128)(2,1)S(1)} copy-done((bf16[512,1280]{1,0:T(8,128)(2,1)S(1)}, bf16[512,1280]{1,0:T(8,128)(2,1)}, u32[]{:S(2)}) %copy-start.1) | copy-done | bytes 1310744
  6.7 0.0 copy-start.2
  6.7 0.9 copy-done.2
  7.5 0.0 copy-start.3
  7.5 0.7 copy-done.3
  8.2 0.0 copy-start.4
  8.2 0.7 copy-done.4
  8.9 0.0 copy-start.5
  8.9 0.7 copy-done.5
  9.6 0.0 copy-start.6
  9.6 43.1 %route_and_encode.1.slab_ref = bf16[8,64,256]{2,1,0:T(8,128)(2,1)S(1)} custom-call(s32[8,32]{1,0:T(8,128)S(1)} %bitcast.5, bf16[1,30,1280]{2,1,0:T(8,128)(2,1)S(1)} %copy-done.2, bf16[16,512]{1,0:T(8,128)(2,1)S(1)} %concatenate.3.w0_ref, f32[7,512]{1,0:T(8,128)S(1)} %get-tuple-element.6.gain_ref, f32[7,512]{1,0:T(8,128)S(1)} %get-tuple-element.5.shift_ref, ...), custom_call_target="tpu_custom_call" | custom-call | tf_op jit(solution)/shard_map/route_and_encode/pallas_call | solution.py:192
  52.7 0.0 copy-done.6
  52.7 6.9 %copy.14 = bf16[2,128,80,80]{3,2,1,0:T(8,128)(2,1)} copy(bf16[2,128,80,80]{1,3,2,0:T(8,128)(2,1)S(1)} %copy-done.6) | data formatting | bytes 6553600 | tf_op args[11]
  59.7 6.2 %pad.15.wb_hbm = bf16[2,10656,128]{2,1,0:T(8,128)(2,1)} pad(bf16[2,10240,80]{2,1,0:T(8,128)(2,1)} %bitcast.8, bf16[]{:T(256)} %constant.7.clone.1), padding=0_0x80_336x0_48 | pad | bytes 8732674 | tf_op jit(solution)/shard_map/jit(_pad)/pad | solution.py:322
  65.8 32.1 %positional_conv.1 = bf16[1,64,1280]{2,1,0:T(8,128)(2,1)S(1)} custom-call(bf16[8,64,256]{2,1,0:T(8,128)(2,1)S(1)} %route_and_encode.1.slab_ref, f32[8,128]{1,0:T(8,128)S(1)} %pad.13.lens_ref, f32[2,1,128]{2,1,0:T(1,128)S(1)} %pad.14.bias_ref, bf16[2,10656,128]{2,1,0:T(8,128)(2,1)} %pad.15.wb_hbm), custom_call_target="tpu_custom_call" | custom-call | tf_op jit(solution)/shard_map/positional_conv/pallas_call | solution.py:323
  97.9 0.7 copy.16
  (2 shorter events, 0.0 us)
Async XLA Ops:
  3.7 1.6 %copy-start = (bf16[2,2,512,512]{3,2,1,0:T(8,128)(2,1)S(1)}, bf16[2,2,512,512]{3,2,1,0:T(8,128)(2,1)}, u32[]{:S(2)}) copy-start(bf16[2,2,512,512]{3,2,1,0:T(8,128)(2,1)} %wl_hbm.1) | copy-start | bytes 6291460
  5.3 1.3 %copy-start.1 = (bf16[512,1280]{1,0:T(8,128)(2,1)S(1)}, bf16[512,1280]{1,0:T(8,128)(2,1)}, u32[]{:S(2)}) copy-start(bf16[512,1280]{1,0:T(8,128)(2,1)} %wp_hbm.1) | copy-start | bytes 3932164
  6.7 0.9 copy-start.2
  7.5 0.7 copy-start.3
  8.2 0.7 copy-start.4
  8.9 0.7 copy-start.5
  9.6 43.1 %copy-start.6 = (bf16[2,128,80,80]{1,3,2,0:T(8,128)(2,1)S(1)}, bf16[2,128,80,80]{1,3,2,0:T(8,128)(2,1)}, u32[]{:S(2)}) copy-start(bf16[2,128,80,80]{1,3,2,0:T(8,128)(2,1)} %param.24) | copy-start | bytes 9830404

commit v2 on v1

v2 whole, which is shorter than its diff:
```python
import jax
import jax.numpy as jnp
from jax import lax
from jax.experimental import pallas as pl
from jax.experimental.pallas import tpu as pltpu
from jax.sharding import PartitionSpec as P

NORM_EPS = 1e-5
R2 = 0.7071067811865476
F32, BF = jnp.float32, jnp.bfloat16
MESH = pl.DeviceIdType.MESH
NDP, NFS = 32, 8


def norm_act(h, gain, shift):
    mean = jnp.sum(h, axis=-1, keepdims=True) * (1.0 / h.shape[-1])
    cen = h - mean
    var = jnp.sum(cen * cen, axis=-1, keepdims=True) * (1.0 / h.shape[-1])
    z = cen * lax.rsqrt(var + NORM_EPS) * gain + shift
    return (z * R2) * (1.0 + lax.erf(z))


WROWS = 133 * 80 + 16
PLAN = ((0, 0, 0), (1, 1, 0), (0, 1, 16), (1, 0, 32))


def encoder_kernel(wave_hbm, lens_hbm, w0_hbm, wm_hbm, wl_hbm, gain_hbm, shift_hbm, pg_hbm, ps_hbm, wp_hbm, pb_hbm, wk_hbm,
                   kb_hbm, out_ref, wave_v, lens_s, lens_v, w0_v, gain_v, shift_v, pg_v, ps_v, pb_v, kb_v, blk, blkb, send1,
                   recv1, send2, recv2, rows, xt, a0, a1, a2, a3, a4, a5, hal, fr, wm, wl, wp, slab, rcv, src, x3, cc, wraw, wt,
                   wb, res, fin, ret, wsem, msem, s1, r1, s2, r2, s3, r3, s4, r4):
    me, col = lax.axis_index("dp"), lax.axis_index("fsdp")
    peers = [(dr, dq) for dr in (0, 1, -1) for dq in range(NFS) if (dr, dq) != (0, 0)]

    def at(dr, dq):
        return {"dp": lax.rem(me + dr + NDP, NDP), "fsdp": lax.rem(col + dq + NFS, NFS)}
    barrier = pltpu.get_barrier_semaphore()
    greet = [{"dp": lax.rem(me + n, NDP)} for n in range(1, NDP)] + [at(dr, dq) for dr, dq in peers if dq]
    for to in greet:
        pl.semaphore_signal(barrier, inc=1, device_id=to, device_id_type=MESH)
    load_wave = pltpu.make_async_copy(wave_hbm, wave_v, msem.at[0])
    load_lens = pltpu.make_async_copy(lens_hbm, lens_s, msem.at[1])
    load_lens_v = pltpu.make_async_copy(lens_hbm, lens_v, msem.at[2])
    weights = [pltpu.make_async_copy(wk_hbm.at[g], wraw.at[g], wsem.at[7 + g]) for g in range(2)]
    pairs = ((w0_hbm, w0_v), (gain_hbm, gain_v), (shift_hbm, shift_v), (pg_hbm, pg_v), (ps_hbm, ps_v), (pb_hbm, pb_v), (kb_hbm, kb_v))
    small = [pltpu.make_async_copy(a, b, msem.at[3 + i]) for i, (a, b) in enumerate(pairs)]
    copies = [pltpu.make_async_copy(wm_hbm.at[i], wm.at[i], wsem.at[i]) for i in range(4)]
    copies += [pltpu.make_async_copy(wl_hbm.at[i], wl.at[i], wsem.at[4 + i]) for i in range(2)]
    copies += [pltpu.make_async_copy(wp_hbm, wp, wsem.at[6])]
    for c in [load_wave, load_lens, weights[0], load_lens_v, weights[1]] + small + copies:
        c.start()

    blk[...] = jnp.zeros((512, 128), F32)
    load_wave.wait()
    wave = wave_v[0].astype(F32)
    for r in range(10):
        blk[pl.ds(r, 30, stride=16), :] = wave[:, 128 * r:128 * r + 128]
    blk[pl.ds(10, 29, stride=16), :] = wave[1:30, 0:128]
    blkb[...] = blk[...].astype(BF).reshape(32, 16, 128)

    load_lens.wait()

    def tally(s, carry):
        total, mine, owners = carry[0], carry[1], carry[2:]
        mine = jnp.where(s == me, total, mine)
        total = total + lens_s[col, s]
        owners = tuple(o + jnp.where(total <= (me + NDP * j) * 1280, 1, 0) for j, o in enumerate(owners))
        return (total, mine) + owners
    zero = jnp.int32(0)
    counted = lax.fori_loop(0, NDP, tally, (zero,) * 18)
    start, owners = counted[1] // 1280, counted[2:]

    for t in range(NDP):
        send1[t] = blkb[(t - start) & 31]

    def turn(g):
        weights[g].wait()
        pad = jnp.zeros((48, 128), F32)

        def one(ii, c):
            for u in range(4):
                i = 4 * ii + u
                wt[pl.ds(i, 128, stride=80), :] = jnp.concatenate([wraw[g, i].astype(F32), pad], axis=0).T
            return c
        lax.fori_loop(0, 20, one, 0)

        def pack(r, c):
            wb[g, pl.ds(pl.multiple_of(80 + r * 512, 16), 512), :] = wt[pl.ds(pl.multiple_of(r * 512, 512), 512), :].astype(BF)
            return c
        lax.fori_loop(0, 20, pack, 0)
        wb[g, 0:80, :] = jnp.zeros((80, 128), BF)
        wb[g, 10320:WROWS, :] = jnp.zeros((WROWS - 10320, 128), BF)
    turn(0)
    recv1[me] = send1[me]
    pl.semaphore_wait(barrier, len(greet))
    first = []
    for n in range(1, NDP):
        to = lax.rem(me + n, NDP)
        c = pltpu.make_async_remote_copy(src_ref=send1.at[to], dst_ref=recv1.at[me], send_sem=s1.at[n],
                                         recv_sem=r1.at[n], device_id={"dp": to}, device_id_type=MESH)
        c.start()
        first.append(c)
    turn(1)
    for c in first:
        c.wait()
    half, slot = me // 16, me % 16
    for j in range(16):
        send2[j] = recv1[jnp.minimum(owners[j], 31)]
    second = []
    for j in range(16):
        to = 2 * j + half
        c = pltpu.make_async_remote_copy(src_ref=send2.at[j], dst_ref=recv2.at[slot], send_sem=s2.at[j],
                                         recv_sem=r2.at[slot], device_id={"dp": to}, device_id_type=MESH)
        second.append((to, c))

        @pl.when(to != me)
        def _():
            c.start()

        @pl.when(to == me)
        def _():
            recv2[slot] = send2[j]

    def spread(a):
        lane = lax.broadcasted_iota(jnp.int32, (768, 128), 1)
        full = src[a].reshape(97, 2, 8, 128)
        ev, od = full[:, 0].reshape(776, 128), full[:, 1].reshape(776, 128)
        for par in range(2):
            f0 = (ev if par == 0 else od)[0:768]
            f1 = od[0:768] if par == 0 else ev[8:776]
            f2 = (ev if par == 0 else od)[8:776]
            t1 = pltpu.roll(f1, 80, 1)
            t2 = pltpu.roll(f2, 32, 1)
            v0 = jnp.where(lane < 80, f0, t1)
            v1 = jnp.where(lane < 32, t1, jnp.where(lane < 112, t2, 0.0))
            v = jnp.concatenate([v0, v1], axis=1)
            x3[a, par, 0] = v.astype(BF)
            x3[a, par, 1, 0:752, :] = v[8:760].astype(BF)

    row = lax.broadcasted_iota(jnp.int32, (NDP, 128), 0)
    lane = lax.broadcasted_iota(jnp.int32, (NDP, 128), 1)
    upper = jnp.where(row <= lane, 1.0, 0.0).astype(BF)
    load_lens_v.wait()
    ends = jnp.dot((lens_v[...].astype(F32) * (1.0 / 320)).astype(BF), upper, preferred_element_type=F32)
    ends = jnp.where(lax.broadcasted_iota(jnp.int32, (8, 128), 1) < NDP, ends, 1e9)
    frame = lax.broadcasted_iota(jnp.int32, (195, 8, 128), 0) + (64 * me - 64)
    past = jnp.where(ends[None] <= frame.astype(F32), 1.0, 0.0)
    clip = jnp.sum(past, axis=2, keepdims=True)
    here, after = clip[0:194], clip[1:195]
    ok = (here == after) & (frame[0:194, :, 0:1] >= 0) & (here < NDP)
    src[2, 0:1552, :] = jnp.broadcast_to(jnp.where(ok, here, -1.0), (194, 8, 128)).reshape(1552, 128)
    spread(2)
    cc[...] = jnp.concatenate([src[2, 512:1024].reshape(32, 2, 8, 128)[:, 0].reshape(256, 128)] * 2, axis=1).astype(BF)
    odd = me % 2
    for i in range(16):
        c = pltpu.make_async_remote_copy(src_ref=send2.at[0], dst_ref=recv2.at[i], send_sem=s2.at[0],
                                         recv_sem=r2.at[i], device_id={"dp": me}, device_id_type=MESH)

        @pl.when(16 * odd + i != me)
        def _():
            c.wait_recv()
    for to, c in second:
        @pl.when(to != me)
        def _():
            c.wait_send()

    rows[...] = recv2[...].astype(F32).reshape(256, 128)
    flat = jnp.concatenate([rows[pl.ds(r, 16, stride=16), :] for r in range(11)], axis=1)
    y = jnp.concatenate([flat[:, 160 * e:160 * e + 256] for e in range(8)], axis=0)
    xt[...] = y.T
    halo = jnp.broadcast_to(rows[250:251, :], (16, 128))
    line = lax.broadcasted_iota(jnp.int32, (16, 128), 0)
    xh = halo
    for p in range(1, 15):
        xh = jnp.where(line == p, pltpu.roll(halo, 128 - 5 * p, 1), xh)

    dn = (((0,), (0,)), ((), ()))
    for c in small:
        c.wait()
    gains, shifts = gain_v[...] * R2, shift_v[...] * R2
    g0, b0 = gains[0:1], shifts[0:1]
    w0 = jnp.concatenate([w0_v[...].astype(F32), jnp.zeros((6, 512), F32)], axis=0).astype(BF)

    def put(li, v):
        for t in range(4):
            hal[li, t, 0:v.shape[0], :] = v[:, 128 * t:128 * t + 128]

    def pick(li, begin, size, stride=1):
        ds = pl.ds(begin, size, stride=stride) if stride > 1 else pl.ds(begin, size)
        return jnp.concatenate([hal[li, t, ds, :] for t in range(4)], axis=1)

    h = jnp.dot(xh[:, 0:16].astype(BF), w0, preferred_element_type=F32)
    hal[...] = jnp.zeros(hal.shape, F32)
    put(0, norm_act(h, g0, b0))

    def l0(i, c):
        win = jnp.concatenate([xt[pl.ds(20 * i + 5 * q, 16), :] for q in range(4)], axis=1).astype(BF)
        h = lax.dot_general(win, w0, dn, preferred_element_type=F32)
        a = norm_act(h, g0, b0).astype(BF).reshape(4, 4, 2, 16, 512)
        for q in range(4):
            a0[4 * i + q] = a[q, :, 0].reshape(64, 512)
            a0[4 * i + q + 32] = a[q, :, 1].reshape(64, 512)
        return c
    lax.fori_loop(0, 8, l0, 0)

    srcs = [a0, a1, a2, a3, a4, a5]
    counts = [32, 16, 8, 4, 2, 1]
    for L in range(1, 7):
        inp, n = srcs[L - 1], counts[L - 1]
        K = 3 if L <= 4 else 2
        G = min(8, n)
        copies[L - 1].wait()
        w = (lambda L=L: wm[L - 1].reshape(1536, 512)) if L <= 4 else (lambda L=L: wl[L - 5].reshape(1024, 512))
        g, s = gains[L:L + 1], shifts[L:L + 1]
        if K == 3:
            v = inp[0].astype(F32)
            inp[2 * n] = jnp.concatenate([v[16:64], v[1:16], pick(L - 1, 0, 1)], axis=0).astype(BF)

        def body(i, c, inp=inp, K=K, G=G, w=w, g=g, s=s, L=L, halo=False):
            taps = []
            for k in range(K):
                lhs = [inp[2 * (G * i + q) + k] for q in range(G)]
                if halo:
                    lhs.append(jnp.concatenate([pick(L - 1, k, 8, 2), jnp.zeros((8, 512), F32)], axis=0).astype(BF))
                taps.append(jnp.concatenate(lhs, axis=0) if len(lhs) > 1 else lhs[0])
            a = norm_act(jnp.dot(jnp.concatenate(taps, axis=1), w(), preferred_element_type=F32), g, s)
            if halo:
                put(L, a[64 * G:64 * G + 8])
            if L == 6:
                return a
            for q in range(G):
                srcs[L][G * i + q] = a[64 * q:64 * q + 64].astype(BF)
            return c
        last = body(0, 0, halo=(L <= 3))
        if n // G > 1:
            lax.fori_loop(1, n // G, body, 0)

    v = last.astype(BF).astype(F32)
    for t in range(4):
        for q in range(4):
            fr[t, pl.ds(q, 16, stride=4), :] = v[16 * q:16 * q + 16, 128 * t:128 * t + 128]
    v = jnp.concatenate([fr[t] for t in range(4)], axis=1)
    mean = jnp.sum(v, axis=-1, keepdims=True) * (1.0 / 512)
    cen = v - mean
    var = jnp.sum(cen * cen, axis=-1, keepdims=True) * (1.0 / 512)
    nf = (cen * lax.rsqrt(var + NORM_EPS) * pg_v[...] + ps_v[...]).astype(BF)
    copies[6].wait()
    pr = jnp.dot(nf, wp[...], preferred_element_type=F32) + jnp.concatenate([pb_v[r:r + 1, :] for r in range(10)], axis=1)
    gap = jnp.zeros((64, 48), F32)
    for q in range(8):
        parts = []
        for g in range(2):
            parts += [pr[:, 160 * q + 80 * g:160 * q + 80 * g + 80], gap]
        slab[q] = jnp.concatenate(parts, axis=1).astype(BF)
    rcv[1, col] = slab[col]
    sends = []
    for n, (dr, dq) in enumerate(peers):
        to = at(dr, dq)
        c = pltpu.make_async_remote_copy(src_ref=slab.at[to["fsdp"]], dst_ref=rcv.at[1 - dr, col],
                                         send_sem=s3.at[n], recv_sem=r3.at[n], device_id=to, device_id_type=MESH)
        c.start()
        sends.append(c)

    flat = jnp.concatenate([kb_v[r:r + 1, :] for r in range(10)] + [jnp.zeros((1, 128), F32)], axis=1)
    bias = []
    for g in range(2):
        b = jnp.zeros((1, 128), F32)
        for q in range(NFS):
            b = jnp.where(col == q, flat[:, 160 * q + 80 * g:160 * q + 80 * g + 128], b)
        bias.append(b)
    for c in sends:
        c.wait()

    for g in range(2):
        src[g, 1536:1552, :] = jnp.zeros((16, 128), F32)
        for part in range(3):
            for c in range(NFS):
                src[g, pl.ds(512 * part + c, 64, stride=8), :] = rcv[part, c, :, 128 * g:128 * g + 128].astype(F32)
    spread(0)
    spread(1)

    def body(i, acc):
        ctr = cc[...]
        at_row = pl.multiple_of(48 * i, 16)
        tap = pl.multiple_of(960 * i, 16)
        masks = [x3[2, par, al, pl.ds(at_row + off, 256), :] == ctr for par, al, off in PLAN]
        out = []
        for g in range(2):
            lhs = jnp.concatenate([
                jnp.where(m, x3[g, par, al, pl.ds(at_row + off, 256), :], jnp.zeros((), BF))
                for m, (par, al, off) in zip(masks, PLAN)], axis=1)
            rhs = jnp.concatenate([
                jnp.concatenate([wb[g, pl.ds(tap + 240 * s + 80, 256), :], wb[g, pl.ds(tap + 240 * s, 256), :]], axis=1)
                for s in range(4)], axis=0)
            out.append(acc[g] + jnp.dot(lhs, rhs, preferred_element_type=F32))
        return tuple(out)
    acc = lax.fori_loop(0, 11, body, (jnp.zeros((256, 256), F32),) * 2)

    for g in range(2):
        halves = []
        for v in range(2):
            pos = acc[g][:, 128 * v:128 * v + 128] + bias[g]
            own = src[g, 512:1024].reshape(32, 2, 8, 128)[:, v].reshape(256, 128)
            mark = src[2, 512:1024].reshape(32, 2, 8, 128)[:, v].reshape(256, 128)
            gel = 0.5 * pos * (1.0 + lax.erf(pos * R2))
            halves.append(jnp.where(mark >= 0.0, own + gel, 0.0).reshape(32, 1, 8, 128))
        res[g] = jnp.concatenate(halves, axis=1).reshape(512, 128)
        for c in range(NFS):
            fin[c, :, 128 * g:128 * g + 128] = res[g, pl.ds(c, 64, stride=8), :].astype(BF)
    ret[col] = fin[col]
    back = []
    for dq in range(1, NFS):
        to = at(0, dq)
        c = pltpu.make_async_remote_copy(src_ref=fin.at[to["fsdp"]], dst_ref=ret.at[col], send_sem=s4.at[dq],
                                         recv_sem=r4.at[dq], device_id=to, device_id_type=MESH)
        c.start()
        back.append(c)
    for c in back:
        c.wait()
    out_ref[0] = jnp.concatenate(
        [ret[q, :, 128 * g:128 * g + 80] for q in range(NFS) for g in range(2)], axis=1)


def per_device(waveform, clip_lengths, conv_first, conv_mid, conv_last, conv_gain, conv_shift, proj_gain, proj_shift,
               proj_weight, proj_bias, pos_weight, pos_bias):
    H = pl.BlockSpec(memory_space=pltpu.HBM)
    D = pltpu.SemaphoreType.DMA
    V = pltpu.VMEM
    return pl.pallas_call(
        encoder_kernel,
        out_shape=jax.ShapeDtypeStruct((1, 64, 1280), BF),
        in_specs=[H] * 13,
        out_specs=pl.BlockSpec(memory_space=pltpu.VMEM),
        scratch_shapes=[V((1, 30, 1280), BF), pltpu.SMEM((8, 32), jnp.int32), V((8, 32), jnp.int32), V((10, 512), BF), V((7, 512), F32),
                        V((7, 512), F32), V((1, 512), F32), V((1, 512), F32), V((10, 128), F32), V((10, 128), F32),
                        V((512, 128), F32), V((32, 16, 128), BF), V((32, 16, 128), BF),
                        V((32, 16, 128), BF), V((16, 16, 128), BF), V((16, 16, 128), BF),
                        V((256, 128), F32), V((256, 128), F32),
                        V((65, 64, 512), BF), V((33, 64, 512), BF), V((17, 64, 512), BF),
                        V((9, 64, 512), BF), V((4, 64, 512), BF), V((2, 64, 512), BF),
                        V((4, 4, 24, 128), F32), V((4, 64, 128), F32),
                        V((4, 3, 512, 512), BF), V((2, 2, 512, 512), BF), V((512, 1280), BF),
                        V((8, 64, 256), BF), V((3, 8, 64, 256), BF), V((3, 1552, 128), F32), V((3, 2, 2, 768, 256), BF),
                        V((256, 256), BF), V((2, 80, 80, 128), BF), V((10240, 128), F32), V((2, WROWS, 128), BF), V((2, 512, 128), F32),
                        V((8, 64, 256), BF), V((8, 64, 256), BF),
                        D((9,)), D((10,)), D((32,)), D((32,)), D((16,)), D((16,)), D((23,)), D((23,)), D((8,)), D((8,))],
        compiler_params=pltpu.CompilerParams(vmem_limit_bytes=62 << 20, collective_id=0, has_side_effects=True),
        name="encoder",
    )(waveform, clip_lengths[:, :, 0], conv_first, conv_mid, conv_last, conv_gain, conv_shift, proj_gain[None], proj_shift[None],
      proj_weight, proj_bias.reshape(10, 128), jnp.transpose(pos_weight, (0, 2, 3, 1)), pos_bias.reshape(10, 128))


def solution(mesh):
    return jax.shard_map(
        per_device,
        mesh=mesh,
        in_specs=(P("fsdp", "dp", None),) + (P(),) * 10 + (P("fsdp", None, None, None), P()),
        out_specs=P("fsdp", "dp", None),
        check_vma=False,
    )
```

time: 99.2 us -> 67.9 us (0.68)
  local copies, waits for them, and re-layouts: 21.9 us -> 1.59 us
  Pallas kernels: 75.2 us -> 66.2 us
  other arithmetic: 1.44 us -> 0 us
    unnamed x16 -> x1, local copies, waits for them, and re-layouts: 13.4 us -> 1.59 us
    pallas_call x2 -> x1, Pallas kernels: 75.2 us -> 66.2 us  [per_device(): pl.pallas_call(encoder_kernel, out_shape=jax.ShapeDtypeStruct((1, 64, 128...]
    pad x3 -> x0, local copies, waits for them, and re-layouts: 6.19 us -> none  [the longest x1 6.18 us: pos_call(): wb = jnp.pad(w, ((0, 0), (80, WROWS - 80 - 10240), (0, 48)))]
where the time goes in v2:
time: 67.9 us; the launch traced here: 67.8 us
  Pallas kernels  66.2 us (97%)
  local copies, waits for them, and re-layouts  1.59 us (2%)
    pallas_call x1, Pallas kernels, per_device(): pl.pallas_call(encoder_kernel, out_shape=jax.ShapeDtypeStruct((1, 64, 128...  66.2 us
    unnamed x1, local copies, waits for them, and re-layouts  1.59 us

profile of v2, /device:TPU:1, one launch (start us, length us, event | category | flops | bytes accessed | tf_op | source)
XLA Modules:
  0.0 67.8 jit_solution(10098822604112665737)
XLA Ops:
  0.0 66.2 %encoder.1 = bf16[1,64,1280]{2,1,0:T(8,128)(2,1)} custom-call(bf16[1,30,1280]{2,1,0:T(8,128)(2,1)} %wave_hbm.1, s32[8,32]{1,0:T(8,128)} %bitcast.9, bf16[10,512]{1,0:T(8,128)(2,1)} %w0_hbm.1, bf16[4,3,512,512]{3,2,1,0:T(8,128)(2,1)} %wm_hbm.1, bf16[2,2,512,512]{3,2,1,0:T(8,128)(2,1)} %wl_hbm.1, f32[7,512]{1,0:T(8,128)} %gain_hbm.1, f32[7,512]{1,0:T(8,128)} %shift_hbm.1, ...), custom_call_target="tpu_custom_call" | custom-call | tf_op jit(solution)/shard_map/encoder/pallas_call | solution.py:328
  66.2 1.6 %copy.15 = bf16[1,64,1280]{2,1,0:T(8,128)(2,1)} copy(bf16[1,64,1280]{2,1,0:T(8,128)(2,1)} %encoder.1) | data formatting | bytes 327680

commit v3 on v2

--- a/solution.py
+++ b/solution.py
@@ -20,6 +20,7 @@
     return (z * R2) * (1.0 + lax.erf(z))
 
 
+VMEM_MB = 58
 WROWS = 133 * 80 + 16
 PLAN = ((0, 0, 0), (1, 1, 0), (0, 1, 16), (1, 0, 32))
 
@@ -27,14 +28,22 @@
 def encoder_kernel(wave_hbm, lens_hbm, w0_hbm, wm_hbm, wl_hbm, gain_hbm, shift_hbm, pg_hbm, ps_hbm, wp_hbm, pb_hbm, wk_hbm,
                    kb_hbm, out_ref, wave_v, lens_s, lens_v, w0_v, gain_v, shift_v, pg_v, ps_v, pb_v, kb_v, blk, blkb, send1,
                    recv1, send2, recv2, rows, xt, a0, a1, a2, a3, a4, a5, hal, fr, wm, wl, wp, slab, rcv, src, x3, cc, wraw, wt,
-                   wb, res, fin, ret, wsem, msem, s1, r1, s2, r2, s3, r3, s4, r4):
+                   wb, res, fin, ret, part, wsem, msem, s1, r1, s2, r2, s3, r3, s4, r4):
     me, col = lax.axis_index("dp"), lax.axis_index("fsdp")
-    peers = [(dr, dq) for dr in (0, 1, -1) for dq in range(NFS) if (dr, dq) != (0, 0)]
+    peers = [(dr, dq) for dr in (0, 1, -1) for dq in (4, 5, 3, 6, 2, 7, 1, 0) if (dr, dq) != (0, 0)]
+    steps = sorted([(dz, dy) for dz in range(8) for dy in range(4) if dz or dy],
+                   key=lambda s: -(min(s[0], 8 - s[0]) + min(s[1], 4 - s[1])))
 
     def at(dr, dq):
-        return {"dp": lax.rem(me + dr + NDP, NDP), "fsdp": lax.rem(col + dq + NFS, NFS)}
+        return {"dp": (me + dr) & (NDP - 1), "fsdp": (col + dq) & (NFS - 1)}
+
+    def hop(dz, dy):
+        return (((me >> 2) + dz) & 7) * 4 + ((me + dy) & 3)
+
+    def residue(d):
+        return 16 * (1 - (d & 1)) + 2 * (d >> 2) + ((d & 3) >> 1)
     barrier = pltpu.get_barrier_semaphore()
-    greet = [{"dp": lax.rem(me + n, NDP)} for n in range(1, NDP)] + [at(dr, dq) for dr, dq in peers if dq]
+    greet = [{"dp": hop(dz, dy)} for dz, dy in steps] + [at(dr, dq) for dr, dq in peers if dq]
     for to in greet:
         pl.semaphore_signal(barrier, inc=1, device_id=to, device_id_type=MESH)
     load_wave = pltpu.make_async_copy(wave_hbm, wave_v, msem.at[0])
@@ -59,18 +68,20 @@
 
     load_lens.wait()
 
+    mine_mod = residue(me)
+
     def tally(s, carry):
         total, mine, owners = carry[0], carry[1], carry[2:]
         mine = jnp.where(s == me, total, mine)
         total = total + lens_s[col, s]
-        owners = tuple(o + jnp.where(total <= (me + NDP * j) * 1280, 1, 0) for j, o in enumerate(owners))
+        owners = tuple(o + jnp.where(total <= (mine_mod + NDP * j) * 1280, 1, 0) for j, o in enumerate(owners))
         return (total, mine) + owners
     zero = jnp.int32(0)
     counted = lax.fori_loop(0, NDP, tally, (zero,) * 18)
     start, owners = counted[1] // 1280, counted[2:]
 
     for t in range(NDP):
-        send1[t] = blkb[(t - start) & 31]
+        send1[t] = blkb[(residue(t) - start) & 31]
 
     def turn(g):
         weights[g].wait()
@@ -93,8 +104,8 @@
     recv1[me] = send1[me]
     pl.semaphore_wait(barrier, len(greet))
     first = []
-    for n in range(1, NDP):
-        to = lax.rem(me + n, NDP)
+    for n, (dz, dy) in enumerate(steps):
+        to = hop(dz, dy)
         c = pltpu.make_async_remote_copy(src_ref=send1.at[to], dst_ref=recv1.at[me], send_sem=s1.at[n],
                                          recv_sem=r1.at[n], device_id={"dp": to}, device_id_type=MESH)
         c.start()
@@ -102,39 +113,37 @@
     turn(1)
     for c in first:
         c.wait()
-    half, slot = me // 16, me % 16
+    half, slot = mine_mod >> 4, mine_mod & 15
     for j in range(16):
         send2[j] = recv1[jnp.minimum(owners[j], 31)]
     second = []
-    for j in range(16):
-        to = 2 * j + half
-        c = pltpu.make_async_remote_copy(src_ref=send2.at[j], dst_ref=recv2.at[slot], send_sem=s2.at[j],
-                                         recv_sem=r2.at[slot], device_id={"dp": to}, device_id_type=MESH)
-        second.append((to, c))
-
-        @pl.when(to != me)
-        def _():
+    for n in (4, 3, 5, 2, 6, 1, 7, 0):
+        for m in range(2):
+            j = (((me >> 2) + n) & 7) * 2 + m
+            to = 2 * j + half
+            c = pltpu.make_async_remote_copy(src_ref=send2.at[j], dst_ref=recv2.at[slot], send_sem=s2.at[j],
+                                             recv_sem=r2.at[slot], device_id={"dp": to}, device_id_type=MESH)
             c.start()
-
-        @pl.when(to == me)
-        def _():
-            recv2[slot] = send2[j]
-
-    def spread(a):
-        lane = lax.broadcasted_iota(jnp.int32, (768, 128), 1)
-        full = src[a].reshape(97, 2, 8, 128)
-        ev, od = full[:, 0].reshape(776, 128), full[:, 1].reshape(776, 128)
+            second.append(c)
+
+    def spread(a, lo, hi):
+        n = hi - lo + (1 if hi < 96 else 0)
+        lane = lax.broadcasted_iota(jnp.int32, (8 * n, 128), 1)
+        full = src[a, 16 * lo:16 * (lo + n + 1), :].reshape(n + 1, 2, 8, 128)
+        ev, od = full[:, 0].reshape(8 * n + 8, 128), full[:, 1].reshape(8 * n + 8, 128)
         for par in range(2):
-            f0 = (ev if par == 0 else od)[0:768]
-            f1 = od[0:768] if par == 0 else ev[8:776]
-            f2 = (ev if par == 0 else od)[8:776]
+            f0 = (ev if par == 0 else od)[0:8 * n]
+            f1 = od[0:8 * n] if par == 0 else ev[8:8 * n + 8]
+            f2 = (ev if par == 0 else od)[8:8 * n + 8]
             t1 = pltpu.roll(f1, 80, 1)
             t2 = pltpu.roll(f2, 32, 1)
             v0 = jnp.where(lane < 80, f0, t1)
             v1 = jnp.where(lane < 32, t1, jnp.where(lane < 112, t2, 0.0))
             v = jnp.concatenate([v0, v1], axis=1)
-            x3[a, par, 0] = v.astype(BF)
-            x3[a, par, 1, 0:752, :] = v[8:760].astype(BF)
+            m = 8 * (hi - lo)
+            x3[a, par, 0, 8 * lo:8 * lo + m, :] = v[0:m].astype(BF)
+            k = m if hi < 96 else m - 16
+            x3[a, par, 1, 8 * lo:8 * lo + k, :] = v[8:8 + k].astype(BF)
 
     row = lax.broadcasted_iota(jnp.int32, (NDP, 128), 0)
     lane = lax.broadcasted_iota(jnp.int32, (NDP, 128), 1)
@@ -148,20 +157,13 @@
     here, after = clip[0:194], clip[1:195]
     ok = (here == after) & (frame[0:194, :, 0:1] >= 0) & (here < NDP)
     src[2, 0:1552, :] = jnp.broadcast_to(jnp.where(ok, here, -1.0), (194, 8, 128)).reshape(1552, 128)
-    spread(2)
+    spread(2, 0, 96)
     cc[...] = jnp.concatenate([src[2, 512:1024].reshape(32, 2, 8, 128)[:, 0].reshape(256, 128)] * 2, axis=1).astype(BF)
-    odd = me % 2
     for i in range(16):
-        c = pltpu.make_async_remote_copy(src_ref=send2.at[0], dst_ref=recv2.at[i], send_sem=s2.at[0],
-                                         recv_sem=r2.at[i], device_id={"dp": me}, device_id_type=MESH)
-
-        @pl.when(16 * odd + i != me)
-        def _():
-            c.wait_recv()
-    for to, c in second:
-        @pl.when(to != me)
-        def _():
-            c.wait_send()
+        pltpu.make_async_remote_copy(src_ref=send2.at[0], dst_ref=recv2.at[i], send_sem=s2.at[0],
+                                     recv_sem=r2.at[i], device_id={"dp": me}, device_id_type=MESH).wait_recv()
+    for c in second:
+        c.wait_send()
 
     rows[...] = recv2[...].astype(F32).reshape(256, 128)
     flat = jnp.concatenate([rows[pl.ds(r, 16, stride=16), :] for r in range(11)], axis=1)
@@ -245,12 +247,10 @@
     nf = (cen * lax.rsqrt(var + NORM_EPS) * pg_v[...] + ps_v[...]).astype(BF)
     copies[6].wait()
     pr = jnp.dot(nf, wp[...], preferred_element_type=F32) + jnp.concatenate([pb_v[r:r + 1, :] for r in range(10)], axis=1)
-    gap = jnp.zeros((64, 48), F32)
     for q in range(8):
-        parts = []
-        for g in range(2):
-            parts += [pr[:, 160 * q + 80 * g:160 * q + 80 * g + 80], gap]
-        slab[q] = jnp.concatenate(parts, axis=1).astype(BF)
+        v = pr[:, 160 * q:160 * q + 160]
+        rest = jnp.concatenate([v[16 * b:16 * b + 16, 128:160] for b in range(4)], axis=1)
+        slab[q] = jnp.concatenate([v[:, 0:128], rest], axis=0).astype(BF)
     rcv[1, col] = slab[col]
     sends = []
     for n, (dr, dq) in enumerate(peers):
@@ -267,57 +267,73 @@
         for q in range(NFS):
             b = jnp.where(col == q, flat[:, 160 * q + 80 * g:160 * q + 80 * g + 128], b)
         bias.append(b)
-    for c in sends:
-        c.wait()
-
+    low = lax.broadcasted_iota(jnp.int32, (64, 128), 1) < 48
+
+    def interleave(part):
+        for c in range(NFS):
+            v = rcv[part, c].astype(F32)
+            rest = jnp.concatenate([pltpu.roll(v[64:80], (176 - 32 * b) & 127, 1) for b in range(4)], axis=0)
+            src[0, pl.ds(512 * part + c, 64, stride=8), :] = v[0:64]
+            src[1, pl.ds(512 * part + c, 64, stride=8), :] = jnp.where(low, pltpu.roll(v[0:64], 48, 1), rest)
     for g in range(2):
         src[g, 1536:1552, :] = jnp.zeros((16, 128), F32)
-        for part in range(3):
-            for c in range(NFS):
-                src[g, pl.ds(512 * part + c, 64, stride=8), :] = rcv[part, c, :, 128 * g:128 * g + 128].astype(F32)
-    spread(0)
-    spread(1)
-
-    def body(i, acc):
-        ctr = cc[...]
-        at_row = pl.multiple_of(48 * i, 16)
-        tap = pl.multiple_of(960 * i, 16)
-        masks = [x3[2, par, al, pl.ds(at_row + off, 256), :] == ctr for par, al, off in PLAN]
-        out = []
-        for g in range(2):
-            lhs = jnp.concatenate([
-                jnp.where(m, x3[g, par, al, pl.ds(at_row + off, 256), :], jnp.zeros((), BF))
-                for m, (par, al, off) in zip(masks, PLAN)], axis=1)
-            rhs = jnp.concatenate([
-                jnp.concatenate([wb[g, pl.ds(tap + 240 * s + 80, 256), :], wb[g, pl.ds(tap + 240 * s, 256), :]], axis=1)
-                for s in range(4)], axis=0)
-            out.append(acc[g] + jnp.dot(lhs, rhs, preferred_element_type=F32))
-        return tuple(out)
-    acc = lax.fori_loop(0, 11, body, (jnp.zeros((256, 256), F32),) * 2)
-
-    for g in range(2):
+    for c in sends[0:15]:
+        c.wait_recv()
+    interleave(0)
+    interleave(1)
+    for g in range(2):
+        spread(g, 0, 60)
+
+    def taps(groups):
+        def body(i, acc):
+            ctr = cc[...]
+            at_row = pl.multiple_of(48 * i, 16)
+            tap = pl.multiple_of(960 * i, 16)
+            masks = [x3[2, par, al, pl.ds(at_row + off, 256), :] == ctr for par, al, off in PLAN]
+            out = []
+            for n, g in enumerate(groups):
+                lhs = jnp.concatenate([
+                    jnp.where(m, x3[g, par, al, pl.ds(at_row + off, 256), :], jnp.zeros((), BF))
+                    for m, (par, al, off) in zip(masks, PLAN)], axis=1)
+                rhs = jnp.concatenate([
+                    jnp.concatenate([wb[g, pl.ds(tap + 240 * s + 80, 256), :], wb[g, pl.ds(tap + 240 * s, 256), :]], axis=1)
+                    for s in range(4)], axis=0)
+                out.append(acc[n] + jnp.dot(lhs, rhs, preferred_element_type=F32))
+            return tuple(out)
+        return body
+    acc = lax.fori_loop(0, 5, taps((0, 1)), (jnp.zeros((256, 256), F32),) * 2)
+    part[...] = acc[1]
+    for c in sends[15:23]:
+        c.wait_recv()
+    interleave(2)
+    for g in range(2):
+        spread(g, 60, 96)
+
+    back = []
+    for g in range(2):
+        a = lax.fori_loop(5, 11, taps((g,)), ((acc[0] if g == 0 else part[...]),))[0]
         halves = []
         for v in range(2):
-            pos = acc[g][:, 128 * v:128 * v + 128] + bias[g]
+            pos = a[:, 128 * v:128 * v + 128] + bias[g]
             own = src[g, 512:1024].reshape(32, 2, 8, 128)[:, v].reshape(256, 128)
             mark = src[2, 512:1024].reshape(32, 2, 8, 128)[:, v].reshape(256, 128)
             gel = 0.5 * pos * (1.0 + lax.erf(pos * R2))
             halves.append(jnp.where(mark >= 0.0, own + gel, 0.0).reshape(32, 1, 8, 128))
         res[g] = jnp.concatenate(halves, axis=1).reshape(512, 128)
         for c in range(NFS):
-            fin[c, :, 128 * g:128 * g + 128] = res[g, pl.ds(c, 64, stride=8), :].astype(BF)
-    ret[col] = fin[col]
-    back = []
-    for dq in range(1, NFS):
-        to = at(0, dq)
-        c = pltpu.make_async_remote_copy(src_ref=fin.at[to["fsdp"]], dst_ref=ret.at[col], send_sem=s4.at[dq],
-                                         recv_sem=r4.at[dq], device_id=to, device_id_type=MESH)
-        c.start()
-        back.append(c)
+            fin[g, c] = res[g, pl.ds(c, 64, stride=8), :].astype(BF)
+        ret[g, col] = fin[g, col]
+        for n, dq in enumerate((4, 5, 3, 6, 2, 7, 1)):
+            to = at(0, dq)
+            c = pltpu.make_async_remote_copy(src_ref=fin.at[g, to["fsdp"]], dst_ref=ret.at[g, col], send_sem=s4.at[g, n],
+                                             recv_sem=r4.at[g, n], device_id=to, device_id_type=MESH)
+            c.start()
+            back.append(c)
+    for c in sends:
+        c.wait_send()
     for c in back:
         c.wait()
-    out_ref[0] = jnp.concatenate(
-        [ret[q, :, 128 * g:128 * g + 80] for q in range(NFS) for g in range(2)], axis=1)
+    out_ref[0] = jnp.concatenate([ret[g, q, :, 0:80] for q in range(NFS) for g in range(2)], axis=1)
 
 
 def per_device(waveform, clip_lengths, conv_first, conv_mid, conv_last, conv_gain, conv_shift, proj_gain, proj_shift,
@@ -339,11 +355,11 @@
                         V((9, 64, 512), BF), V((4, 64, 512), BF), V((2, 64, 512), BF),
                         V((4, 4, 24, 128), F32), V((4, 64, 128), F32),
                         V((4, 3, 512, 512), BF), V((2, 2, 512, 512), BF), V((512, 1280), BF),
-                        V((8, 64, 256), BF), V((3, 8, 64, 256), BF), V((3, 1552, 128), F32), V((3, 2, 2, 768, 256), BF),
+                        V((8, 80, 128), BF), V((3, 8, 80, 128), BF), V((3, 1552, 128), F32), V((3, 2, 2, 768, 256), BF),
                         V((256, 256), BF), V((2, 80, 80, 128), BF), V((10240, 128), F32), V((2, WROWS, 128), BF), V((2, 512, 128), F32),
-                        V((8, 64, 256), BF), V((8, 64, 256), BF),
-                        D((9,)), D((10,)), D((32,)), D((32,)), D((16,)), D((16,)), D((23,)), D((23,)), D((8,)), D((8,))],
-        compiler_params=pltpu.CompilerParams(vmem_limit_bytes=62 << 20, collective_id=0, has_side_effects=True),
+                        V((2, 8, 64, 128), BF), V((2, 8, 64, 128), BF), V((256, 256), F32),
+                        D((9,)), D((10,)), D((32,)), D((32,)), D((16,)), D((16,)), D((23,)), D((23,)), D((2, 7)), D((2, 7))],
+        compiler_params=pltpu.CompilerParams(vmem_limit_bytes=VMEM_MB << 20, collective_id=0, has_side_effects=True),
         name="encoder",
     )(waveform, clip_lengths[:, :, 0], conv_first, conv_mid, conv_last, conv_gain, conv_shift, proj_gain[None], proj_shift[None],
       proj_weight, proj_bias.reshape(10, 128), jnp.transpose(pos_weight, (0, 2, 3, 1)), pos_bias.reshape(10, 128))

time: 67.9 us -> 65.2 us (0.960)
  Pallas kernels: 66.2 us -> 63.5 us
    pallas_call x1, Pallas kernels: 66.2 us -> 63.5 us  [per_device(): pl.pallas_call(encoder_kernel, out_shape=jax.ShapeDtypeStruct((1, 64, 128...]
where the time goes in v3:
time: 65.2 us; the launch traced here: 65.1 us
  Pallas kernels  63.5 us (97%)
  local copies, waits for them, and re-layouts  1.59 us (2%)
    pallas_call x1, Pallas kernels, per_device(): pl.pallas_call(encoder_kernel, out_shape=jax.ShapeDtypeStruct((1, 64, 128...  63.5 us
    unnamed x1, local copies, waits for them, and re-layouts  1.59 us

profile of v3, /device:TPU:1, one launch (start us, length us, event | category | flops | bytes accessed | tf_op | source)
XLA Modules:
  0.0 65.1 jit_solution(17112336411127336380)
XLA Ops:
  0.0 63.5 %encoder.1 = bf16[1,64,1280]{2,1,0:T(8,128)(2,1)} custom-call(bf16[1,30,1280]{2,1,0:T(8,128)(2,1)} %wave_hbm.1, s32[8,32]{1,0:T(8,128)} %bitcast.9, bf16[10,512]{1,0:T(8,128)(2,1)} %w0_hbm.1, bf16[4,3,512,512]{3,2,1,0:T(8,128)(2,1)} %wm_hbm.1, bf16[2,2,512,512]{3,2,1,0:T(8,128)(2,1)} %wl_hbm.1, f32[7,512]{1,0:T(8,128)} %gain_hbm.1, f32[7,512]{1,0:T(8,128)} %shift_hbm.1, ...), custom_call_target="tpu_custom_call" | custom-call | tf_op jit(solution)/shard_map/encoder/pallas_call | solution.py:344
  63.5 1.6 %copy.15 = bf16[1,64,1280]{2,1,0:T(8,128)(2,1)} copy(bf16[1,64,1280]{2,1,0:T(8,128)(2,1)} %encoder.1) | data formatting | bytes 327680

commit v4 on v3

--- a/solution.py
+++ b/solution.py
@@ -12,12 +12,10 @@
 NDP, NFS = 32, 8
 
 
-def norm_act(h, gain, shift):
-    mean = jnp.sum(h, axis=-1, keepdims=True) * (1.0 / h.shape[-1])
-    cen = h - mean
-    var = jnp.sum(cen * cen, axis=-1, keepdims=True) * (1.0 / h.shape[-1])
-    z = cen * lax.rsqrt(var + NORM_EPS) * gain + shift
-    return (z * R2) * (1.0 + lax.erf(z))
+def norm_act(h, gain, shift, eps):
+    var = jnp.sum(h * h, axis=-1, keepdims=True) * (1.0 / h.shape[-1])
+    z = h * lax.rsqrt(var + eps) * gain + shift
+    return z + z * lax.erf(z)
 
 
 VMEM_MB = 58
@@ -83,6 +81,17 @@
     for t in range(NDP):
         send1[t] = blkb[(residue(t) - start) & 31]
 
+    def centre(layer):
+        copies[layer - 1].wait()
+        ref, n, taps = (wm, layer - 1, 3) if layer <= 4 else (wl, layer - 5, 2)
+
+        def one(i, c):
+            at_row = pl.ds(pl.multiple_of(128 * (i & 3), 128), 128)
+            v = ref[n, i >> 2, at_row, :].astype(F32)
+            ref[n, i >> 2, at_row, :] = (v - jnp.sum(v, axis=-1, keepdims=True) * (1.0 / 512)).astype(BF)
+            return c
+        lax.fori_loop(0, 4 * taps, one, 0)
+
     def turn(g):
         weights[g].wait()
         pad = jnp.zeros((48, 128), F32)
@@ -100,7 +109,7 @@
         lax.fori_loop(0, 20, pack, 0)
         wb[g, 0:80, :] = jnp.zeros((80, 128), BF)
         wb[g, 10320:WROWS, :] = jnp.zeros((WROWS - 10320, 128), BF)
-    turn(0)
+    centre(1)
     recv1[me] = send1[me]
     pl.semaphore_wait(barrier, len(greet))
     first = []
@@ -110,7 +119,7 @@
                                          recv_sem=r1.at[n], device_id={"dp": to}, device_id_type=MESH)
         c.start()
         first.append(c)
-    turn(1)
+    turn(0)
     for c in first:
         c.wait()
     half, slot = mine_mod >> 4, mine_mod & 15
@@ -158,6 +167,8 @@
     ok = (here == after) & (frame[0:194, :, 0:1] >= 0) & (here < NDP)
     src[2, 0:1552, :] = jnp.broadcast_to(jnp.where(ok, here, -1.0), (194, 8, 128)).reshape(1552, 128)
     spread(2, 0, 96)
+    for layer in range(2, 7):
+        centre(layer)
     cc[...] = jnp.concatenate([src[2, 512:1024].reshape(32, 2, 8, 128)[:, 0].reshape(256, 128)] * 2, axis=1).astype(BF)
     for i in range(16):
         pltpu.make_async_remote_copy(src_ref=send2.at[0], dst_ref=recv2.at[i], send_sem=s2.at[0],
@@ -180,7 +191,9 @@
         c.wait()
     gains, shifts = gain_v[...] * R2, shift_v[...] * R2
     g0, b0 = gains[0:1], shifts[0:1]
-    w0 = jnp.concatenate([w0_v[...].astype(F32), jnp.zeros((6, 512), F32)], axis=0).astype(BF)
+    w0 = w0_v[...].astype(F32)
+    w0 = w0 - jnp.sum(w0, axis=-1, keepdims=True) * (1.0 / 512)
+    w0 = jnp.concatenate([w0, jnp.zeros((6, 512), F32)], axis=0).astype(BF)
 
     def put(li, v):
         for t in range(4):
@@ -192,12 +205,12 @@
 
     h = jnp.dot(xh[:, 0:16].astype(BF), w0, preferred_element_type=F32)
     hal[...] = jnp.zeros(hal.shape, F32)
-    put(0, norm_act(h, g0, b0))
+    put(0, norm_act(h, g0, b0, NORM_EPS))
 
     def l0(i, c):
         win = jnp.concatenate([xt[pl.ds(20 * i + 5 * q, 16), :] for q in range(4)], axis=1).astype(BF)
         h = lax.dot_general(win, w0, dn, preferred_element_type=F32)
-        a = norm_act(h, g0, b0).astype(BF).reshape(4, 4, 2, 16, 512)
+        a = norm_act(h, g0, b0, NORM_EPS).astype(BF).reshape(4, 4, 2, 16, 512)
         for q in range(4):
             a0[4 * i + q] = a[q, :, 0].reshape(64, 512)
             a0[4 * i + q + 32] = a[q, :, 1].reshape(64, 512)
@@ -210,7 +223,6 @@
         inp, n = srcs[L - 1], counts[L - 1]
         K = 3 if L <= 4 else 2
         G = min(8, n)
-        copies[L - 1].wait()
         w = (lambda L=L: wm[L - 1].reshape(1536, 512)) if L <= 4 else (lambda L=L: wl[L - 5].reshape(1024, 512))
         g, s = gains[L:L + 1], shifts[L:L + 1]
         if K == 3:
@@ -224,7 +236,7 @@
                 if halo:
                     lhs.append(jnp.concatenate([pick(L - 1, k, 8, 2), jnp.zeros((8, 512), F32)], axis=0).astype(BF))
                 taps.append(jnp.concatenate(lhs, axis=0) if len(lhs) > 1 else lhs[0])
-            a = norm_act(jnp.dot(jnp.concatenate(taps, axis=1), w(), preferred_element_type=F32), g, s)
+            a = norm_act(jnp.dot(jnp.concatenate(taps, axis=1), w(), preferred_element_type=F32), g, s, 2 * NORM_EPS)
             if halo:
                 put(L, a[64 * G:64 * G + 8])
             if L == 6:
@@ -244,7 +256,7 @@
     mean = jnp.sum(v, axis=-1, keepdims=True) * (1.0 / 512)
     cen = v - mean
     var = jnp.sum(cen * cen, axis=-1, keepdims=True) * (1.0 / 512)
-    nf = (cen * lax.rsqrt(var + NORM_EPS) * pg_v[...] + ps_v[...]).astype(BF)
+    nf = (cen * lax.rsqrt(var + 2 * NORM_EPS) * pg_v[...] + ps_v[...]).astype(BF)
     copies[6].wait()
     pr = jnp.dot(nf, wp[...], preferred_element_type=F32) + jnp.concatenate([pb_v[r:r + 1, :] for r in range(10)], axis=1)
     for q in range(8):
@@ -267,6 +279,7 @@
         for q in range(NFS):
             b = jnp.where(col == q, flat[:, 160 * q + 80 * g:160 * q + 80 * g + 128], b)
         bias.append(b)
+    turn(1)
     low = lax.broadcasted_iota(jnp.int32, (64, 128), 1) < 48
 
     def interleave(part):

time: 65.2 us -> 61.7 us (0.946)
  Pallas kernels: 63.5 us -> 60 us
    pallas_call x1, Pallas kernels: 63.5 us -> 60 us  [per_device(): pl.pallas_call(encoder_kernel, out_shape=jax.ShapeDtypeStruct((1, 64, 128...]
where the time goes in v4:
time: 61.7 us; the launch traced here: 61.6 us
  Pallas kernels  60 us (97%)
  local copies, waits for them, and re-layouts  1.59 us (3%)
    pallas_call x1, Pallas kernels, per_device(): pl.pallas_call(encoder_kernel, out_shape=jax.ShapeDtypeStruct((1, 64, 128...  60 us
    unnamed x1, local copies, waits for them, and re-layouts  1.59 us

profile of v4, /device:TPU:1, one launch (start us, length us, event | category | flops | bytes accessed | tf_op | source)
XLA Modules:
  0.0 61.6 jit_solution(10821002057878277336)
XLA Ops:
  0.0 60.0 %encoder.1 = bf16[1,64,1280]{2,1,0:T(8,128)(2,1)} custom-call(bf16[1,30,1280]{2,1,0:T(8,128)(2,1)} %wave_hbm.1, s32[8,32]{1,0:T(8,128)} %bitcast.9, bf16[10,512]{1,0:T(8,128)(2,1)} %w0_hbm.1, bf16[4,3,512,512]{3,2,1,0:T(8,128)(2,1)} %wm_hbm.1, bf16[2,2,512,512]{3,2,1,0:T(8,128)(2,1)} %wl_hbm.1, f32[7,512]{1,0:T(8,128)} %gain_hbm.1, f32[7,512]{1,0:T(8,128)} %shift_hbm.1, ...), custom_call_target="tpu_custom_call" | custom-call | tf_op jit(solution)/shard_map/encoder/pallas_call | solution.py:357
  60.0 1.6 %copy.15 = bf16[1,64,1280]{2,1,0:T(8,128)(2,1)} copy(bf16[1,64,1280]{2,1,0:T(8,128)(2,1)} %encoder.1) | data formatting | bytes 327680

commit v5 on v4

--- a/solution.py
+++ b/solution.py
@@ -215,7 +215,7 @@
             a0[4 * i + q] = a[q, :, 0].reshape(64, 512)
             a0[4 * i + q + 32] = a[q, :, 1].reshape(64, 512)
         return c
-    lax.fori_loop(0, 8, l0, 0)
+    lax.fori_loop(0, 8, l0, 0, unroll=True)
 
     srcs = [a0, a1, a2, a3, a4, a5]
     counts = [32, 16, 8, 4, 2, 1]
@@ -246,7 +246,7 @@
             return c
         last = body(0, 0, halo=(L <= 3))
         if n // G > 1:
-            lax.fori_loop(1, n // G, body, 0)
+            lax.fori_loop(1, n // G, body, 0, unroll=True)
 
     v = last.astype(BF).astype(F32)
     for t in range(4):
@@ -314,7 +314,7 @@
                 out.append(acc[n] + jnp.dot(lhs, rhs, preferred_element_type=F32))
             return tuple(out)
         return body
-    acc = lax.fori_loop(0, 5, taps((0, 1)), (jnp.zeros((256, 256), F32),) * 2)
+    acc = lax.fori_loop(0, 5, taps((0, 1)), (jnp.zeros((256, 256), F32),) * 2, unroll=True)
     part[...] = acc[1]
     for c in sends[15:23]:
         c.wait_recv()
@@ -324,7 +324,7 @@
 
     back = []
     for g in range(2):
-        a = lax.fori_loop(5, 11, taps((g,)), ((acc[0] if g == 0 else part[...]),))[0]
+        a = lax.fori_loop(5, 11, taps((g,)), ((acc[0] if g == 0 else part[...]),), unroll=True)[0]
         halves = []
         for v in range(2):
             pos = a[:, 128 * v:128 * v + 128] + bias[g]

time: 61.7 us -> 54.2 us (0.88)
  Pallas kernels: 60 us -> 52.5 us
    pallas_call x1, Pallas kernels: 60 us -> 52.5 us  [per_device(): pl.pallas_call(encoder_kernel, out_shape=jax.ShapeDtypeStruct((1, 64, 128...]
where the time goes in v5:
time: 54.2 us
  Pallas kernels  52.5 us (97%)
  local copies, waits for them, and re-layouts  1.59 us (3%)
    pallas_call x1, Pallas kernels, per_device(): pl.pallas_call(encoder_kernel, out_shape=jax.ShapeDtypeStruct((1, 64, 128...  52.5 us
    unnamed x1, local copies, waits for them, and re-layouts  1.59 us

profile of v5, /device:TPU:1, one launch (start us, length us, event | category | flops | bytes accessed | tf_op | source)
XLA Modules:
  0.0 54.2 jit_solution(9501985517196448557)
XLA Ops:
  0.0 52.5 %encoder.1 = bf16[1,64,1280]{2,1,0:T(8,128)(2,1)} custom-call(bf16[1,30,1280]{2,1,0:T(8,128)(2,1)} %wave_hbm.1, s32[8,32]{1,0:T(8,128)} %bitcast.9, bf16[10,512]{1,0:T(8,128)(2,1)} %w0_hbm.1, bf16[4,3,512,512]{3,2,1,0:T(8,128)(2,1)} %wm_hbm.1, bf16[2,2,512,512]{3,2,1,0:T(8,128)(2,1)} %wl_hbm.1, f32[7,512]{1,0:T(8,128)} %gain_hbm.1, f32[7,512]{1,0:T(8,128)} %shift_hbm.1, ...), custom_call_target="tpu_custom_call" | custom-call | tf_op jit(solution)/shard_map/encoder/pallas_call | solution.py:357
  52.6 1.6 %copy.15 = bf16[1,64,1280]{2,1,0:T(8,128)(2,1)} copy(bf16[1,64,1280]{2,1,0:T(8,128)(2,1)} %encoder.1) | data formatting | bytes 327680

commit v6 on v5

--- a/solution.py
+++ b/solution.py
@@ -290,12 +290,16 @@
             src[1, pl.ds(512 * part + c, 64, stride=8), :] = jnp.where(low, pltpu.roll(v[0:64], 48, 1), rest)
     for g in range(2):
         src[g, 1536:1552, :] = jnp.zeros((16, 128), F32)
-    for c in sends[0:15]:
+    for c in sends[0:7]:
+        c.wait_recv()
+    interleave(1)
+    for g in range(2):
+        spread(g, 32, 60)
+    for c in sends[7:15]:
         c.wait_recv()
     interleave(0)
-    interleave(1)
-    for g in range(2):
-        spread(g, 0, 60)
+    for g in range(2):
+        spread(g, 0, 32)
 
     def taps(groups):
         def body(i, acc):

time: 54.2 us -> 54.1 us (level)
  no operation moved by 1% of the time
where the time goes in v6:
time: 54.1 us; the launch traced here: 54 us
  Pallas kernels  52.4 us (97%)
  local copies, waits for them, and re-layouts  1.59 us (3%)
    pallas_call x1, Pallas kernels, per_device(): pl.pallas_call(encoder_kernel, out_shape=jax.ShapeDtypeStruct((1, 64, 128...  52.4 us
    unnamed x1, local copies, waits for them, and re-layouts  1.59 us

profile of v6, /device:TPU:1, one launch (start us, length us, event | category | flops | bytes accessed | tf_op | source)
XLA Modules:
  0.0 54.0 jit_solution(2472301475945523684)
XLA Ops:
  0.0 52.4 %encoder.1 = bf16[1,64,1280]{2,1,0:T(8,128)(2,1)} custom-call(bf16[1,30,1280]{2,1,0:T(8,128)(2,1)} %wave_hbm.1, s32[8,32]{1,0:T(8,128)} %bitcast.9, bf16[10,512]{1,0:T(8,128)(2,1)} %w0_hbm.1, bf16[4,3,512,512]{3,2,1,0:T(8,128)(2,1)} %wm_hbm.1, bf16[2,2,512,512]{3,2,1,0:T(8,128)(2,1)} %wl_hbm.1, f32[7,512]{1,0:T(8,128)} %gain_hbm.1, f32[7,512]{1,0:T(8,128)} %shift_hbm.1, ...), custom_call_target="tpu_custom_call" | custom-call | tf_op jit(solution)/shard_map/encoder/pallas_call | solution.py:361
  52.4 1.6 %copy.15 = bf16[1,64,1280]{2,1,0:T(8,128)(2,1)} copy(bf16[1,64,1280]{2,1,0:T(8,128)(2,1)} %encoder.1) | data formatting | bytes 327680
